TPU v7x, 128 devices: a whole 4x4x4 slice. The times are simulated.
128 devices in a mesh: row: 8 (over y, core), col: 16 (over z, x).
Axes of the slice: x: 4, y: 4, z: 4, core: 2. Of those that a mesh axis runs over, the one named last changes fastest.
Arguments:
- dealing: int32 [8, 16], P('row'), may hold values from 0 to 15, each once within a row
- residual: bfloat16 [8192, 3072], P('row', 'col'), may hold values from -6 to 6
- queries: bfloat16 [8192, 3072], P('row', 'col'), may hold values from -6 to 6
- draft_keys: bfloat16 [8192, 3072], P('row', 'col'), may hold values from -6 to 6
- draft_values: bfloat16 [8192, 3072], P('row', 'col'), may hold values from -6 to 6
- cache_keys: bfloat16 [128, 1536, 3072], P(('row', 'col')), may hold values from -6 to 6
- cache_values: bfloat16 [128, 1536, 3072], P(('row', 'col')), may hold values from -6 to 6
- cache_lengths: int32 [128], P(('row', 'col')), may hold values from 97 to 1536, as said below
- parents: int32 [128, 64], P(('row', 'col')), may hold values from -1 to 62, as said below
- draft_counts: int32 [128], P(('row', 'col')), may hold values from 32 to 64, as said below
- accepted: int32 [128, 8], P(('row', 'col')), may hold values from -1 to 28, as said below
- out_weight: bfloat16 [3072, 3072], P('row', 'col'), may hold values from -0.109375 to 0.109375
- norm_gain: bfloat16 [3072], P('col'), may hold values from 0.099609375 to 1.8984375
- gate_weight: bfloat16 [3072, 8192], P('row', 'col'), may hold values from -0.109375 to 0.109375
- up_weight: bfloat16 [3072, 8192], P('row', 'col'), may hold values from -0.109375 to 0.109375
- down_weight: bfloat16 [8192, 3072], P('col', 'row'), may hold values from -0.09375 to 0.09375
Outputs:
- layer_out: bfloat16 [8192, 3072], P('row', 'col')
- new_keys: bfloat16 [128, 8, 3072], P(('row', 'col'))
- new_values: bfloat16 [128, 8, 3072], P(('row', 'col'))
Inputs may be any that keep to these rules, and one draw needn't show every extreme that they name: Each row of dealing names every index along col once. `cache_lengths`: the largest is 1536 in every draw. parents[s, 0] = -1, and for i >= 1, i - 4 <= parents[s, i] < i. `draft_counts`: the largest is 64 in every draw. `accepted`: each row lists draft tokens from the root 0 downward, each the child under parents of the one before and below the slot's draft count, then -1; some row fills all 8 entries, and the largest entry is 28 in every draw.
All inputs are finite; a program needn't handle non-finite values.
Results may differ from a plain program's by a relative error of at most 0.017.
Values may be sent and summed in bfloat16 or wider, within the bound.
A program may use at most 128 MiB of HBM per device.

v0:
```python
import math

import jax
import jax.numpy as jnp
from jax import lax
from jax.sharding import PartitionSpec as P

D = 3072
HEADS = 32
HEAD_DIM = 96


def ancestry(parent_row):
    count_all = parent_row.shape[0]
    token_index = jnp.arange(count_all, dtype=jnp.int32)
    linked = jnp.logical_or(
        parent_row[:, None] == token_index[None, :], token_index[:, None] == token_index[None, :]
    )
    ancestors = linked.astype(jnp.float32)
    for sweep in range(max(1, (count_all - 1).bit_length())):
        ancestors = jnp.minimum(jnp.dot(ancestors, ancestors, precision=lax.Precision.HIGHEST), 1.0)
    return ancestors


def rotate(value_rows, position):
    row_count = value_rows.shape[0]
    half_dim = HEAD_DIM // 2
    shaped = value_rows.astype(jnp.float32).reshape(row_count, HEADS, HEAD_DIM)
    frequency = jnp.power(10000.0, -jnp.arange(half_dim, dtype=jnp.float32) * (2.0 / HEAD_DIM))
    angles = position[:, None] * frequency[None, :]
    cosine = jnp.cos(angles)[:, None, :]
    sine_part = jnp.sin(angles)[:, None, :]
    front_half = shaped[..., :half_dim]
    back_half = shaped[..., half_dim:]
    turned = jnp.concatenate(
        [front_half * cosine - back_half * sine_part, back_half * cosine + front_half * sine_part],
        axis=-1,
    )
    return turned.reshape(row_count, HEADS * HEAD_DIM).astype(jnp.bfloat16)


def fold_block(state_now, q_heads, key_block, value_block, allowed):
    running_max, row_totals, accumulator = state_now
    score_scale = 1.0 / math.sqrt(HEAD_DIM)
    key_heads = key_block.reshape(key_block.shape[0], HEADS, HEAD_DIM)
    value_heads = value_block.reshape(value_block.shape[0], HEADS, HEAD_DIM)
    scores = (
        jnp.einsum("qhd,khd->hqk", q_heads, key_heads, preferred_element_type=jnp.float32)
        * score_scale
    )
    scores = jnp.where(allowed[None], scores, -jnp.inf)
    new_max = jnp.maximum(running_max, jnp.max(scores, axis=2))
    rescale = jnp.exp(running_max - new_max)
    weights = jnp.exp(scores - new_max[:, :, None])
    row_totals = row_totals * rescale + jnp.sum(weights, axis=2)
    mixed_rows = jnp.einsum(
        "hqk,khd->qhd",
        weights.astype(jnp.bfloat16),
        value_heads,
        preferred_element_type=jnp.float32,
    )
    accumulator = accumulator * rescale.T[:, :, None] + mixed_rows
    return (new_max, row_totals, accumulator)


def verify_slot(
    query_rows, key_rows, value_rows, cache_k, cache_v, length, parent_row, live_count, path_row
):
    draft_rows = query_rows.shape[0]
    width = query_rows.shape[1]
    ancestors = ancestry(parent_row)
    tree_depth = jnp.sum(ancestors, axis=1) - 1.0
    position = length.astype(jnp.float32) + tree_depth
    q_rot = rotate(query_rows, position)
    k_rot = rotate(key_rows, position)
    q_heads = q_rot.reshape(draft_rows, HEADS, HEAD_DIM)
    cache_rows = cache_k.shape[0]
    block_rows = min(512, cache_rows)

    def cache_step(block_step, state_now):
        block_start = block_step * block_rows
        key_block = lax.dynamic_slice_in_dim(cache_k, block_start, block_rows, 0)
        value_block = lax.dynamic_slice_in_dim(cache_v, block_start, block_rows, 0)
        live_keys = block_start + jnp.arange(block_rows, dtype=jnp.int32) < length
        allowed = jnp.broadcast_to(live_keys[None, :], (draft_rows, block_rows))
        return fold_block(state_now, q_heads, key_block, value_block, allowed)

    initial = (
        jnp.full((HEADS, draft_rows), -jnp.inf, jnp.float32),
        jnp.zeros((HEADS, draft_rows), jnp.float32),
        jnp.zeros((draft_rows, HEADS, HEAD_DIM), jnp.float32),
    )
    block_total = cache_rows // block_rows
    state_now = lax.fori_loop(0, block_total, cache_step, initial)
    token_index = jnp.arange(draft_rows, dtype=jnp.int32)
    allowed = jnp.logical_and(ancestors > 0.5, token_index[None, :] < live_count)
    running_max, row_totals, accumulator = fold_block(
        state_now, q_heads, k_rot, value_rows, allowed
    )
    attended = (
        (accumulator / row_totals.T[:, :, None]).reshape(draft_rows, width).astype(jnp.bfloat16)
    )
    selector = (path_row[:, None] == token_index[None, :]).astype(jnp.bfloat16)
    new_keys = jnp.dot(selector, k_rot, preferred_element_type=jnp.float32).astype(jnp.bfloat16)
    new_values = jnp.dot(selector, value_rows, preferred_element_type=jnp.float32).astype(
        jnp.bfloat16
    )
    return (attended, new_keys, new_values)


def body(
    dealing,
    residual,
    queries,
    draft_keys,
    draft_values,
    cache_keys,
    cache_values,
    cache_lengths,
    parents,
    draft_counts,
    accepted,
    out_weight,
    norm_gain,
    gate_weight,
    up_weight,
    down_weight,
):
    columns = lax.axis_size("col")
    dealt_order = dealing[0]
    rows_here = residual.shape[0]
    draft_rows = rows_here // columns

    def to_slots(block_rows):
        shaped = block_rows.reshape(columns, draft_rows, block_rows.shape[1])
        return jnp.take(shaped, dealt_order, axis=0).reshape(rows_here, block_rows.shape[1])

    mine_q, mine_k, mine_v = (
        lax.all_to_all(to_slots(queries), "col", split_axis=0, concat_axis=1, tiled=True),
        lax.all_to_all(to_slots(draft_keys), "col", split_axis=0, concat_axis=1, tiled=True),
        lax.all_to_all(to_slots(draft_values), "col", split_axis=0, concat_axis=1, tiled=True),
    )
    attended, new_keys, new_values = verify_slot(
        mine_q,
        mine_k,
        mine_v,
        cache_keys[0],
        cache_values[0],
        cache_lengths[0],
        parents[0],
        draft_counts[0],
        accepted[0],
    )
    weight_cols = lax.all_gather(out_weight, "row", axis=0, tiled=True)
    projected = jnp.dot(
        lax.all_gather(attended, "col", axis=0, tiled=True),
        weight_cols,
        preferred_element_type=jnp.float32,
    )
    inverse = jnp.argsort(dealt_order)
    projected = jnp.take(
        projected.reshape(columns, draft_rows, projected.shape[1]), inverse, axis=0
    ).reshape(rows_here, projected.shape[1])
    stream_full = residual.astype(jnp.float32) + projected
    stream = stream_full.astype(jnp.bfloat16)
    stream_wide = lax.optimization_barrier(stream).astype(jnp.float32)
    local_sums = jnp.sum(stream_wide * stream_wide, axis=1)
    row_totals = lax.psum(local_sums, "col")
    factor = lax.rsqrt(row_totals / D + 1e-05)[:, None]
    normed = (stream_wide * factor * norm_gain.astype(jnp.float32)[None, :]).astype(jnp.bfloat16)
    gathered = lax.all_gather(normed, "col", axis=1, tiled=True)
    gate_next = jnp.dot(
        gathered,
        lax.all_gather(gate_weight, "row", axis=0, tiled=True),
        preferred_element_type=jnp.float32,
    )
    up_next = jnp.dot(
        gathered,
        lax.all_gather(up_weight, "row", axis=0, tiled=True),
        preferred_element_type=jnp.float32,
    )
    hidden = (jax.nn.silu(gate_next) * up_next).astype(jnp.bfloat16)
    partial_terms = jnp.dot(
        hidden,
        lax.all_gather(down_weight, "row", axis=1, tiled=True),
        preferred_element_type=jnp.float32,
    )
    summed = lax.psum_scatter(
        partial_terms.astype(jnp.bfloat16), "col", scatter_dimension=1, tiled=True
    ).astype(jnp.float32)
    layer_out = (stream_wide + summed).astype(jnp.bfloat16)
    return (layer_out, new_keys[None], new_values[None])


def solution(mesh):
    placed = (
        P("row", None),
        P("row", "col"),
        P("row", "col"),
        P("row", "col"),
        P("row", "col"),
        P(("row", "col"), None, None),
        P(("row", "col"), None, None),
        P(("row", "col")),
        P(("row", "col"), None),
        P(("row", "col")),
        P(("row", "col"), None),
        P("row", "col"),
        P("col"),
        P("row", "col"),
        P("row", "col"),
        P("col", "row"),
    )
    return jax.shard_map(
        body,
        mesh=mesh,
        in_specs=placed,
        out_specs=(P("row", "col"), P(("row", "col"), None, None), P(("row", "col"), None, None)),
        check_vma=False,
    )
```

profile of v0, /device:TPU:0, one launch (start us, length us, event | category | flops | bytes accessed | tf_op | source)
XLA Modules:
  0.0 458.0 jit_solution(15680085825392630706)
XLA Ops:
  7.2 0.7 compare_select_fusion
  7.9 0.7 compare_and_fusion.1
  8.5 1.2 copy.32
  9.8 1.2 copy.28
  11.0 0.6 gather_fusion.3
  11.6 0.6 gather_fusion.2
  12.4 0.6 gather_fusion.1
  13.0 1.4 broadcast_select_fusion
  14.3 8.0 %all-to-all-start.1 = ((bf16[16,64,192]{2,1,0:T(8,128)(2,1)}), bf16[16,64,192]{2,1,0:T(8,128)(2,1)S(1)}, u32[]{:S(2)}, u32[]{:S(2)}) async-start(bf16[16,64,192]{2,1,0:T(8,128)(2,1)} %get-tuple-element.212), calls=%async_computation.1 | async-start | bytes 1048576 | tf_op jit(solution)/shard_map/all_to_all | solution.py:140
  22.4 0.7 all-gather.9.cloned.1.call-update
  25.6 12.8 %copy.22 = bf16[1,1536,3072]{1,2,0:T(8,128)(2,1)} copy(bf16[1,1536,3072]{2,1,0:T(8,128)(2,1)} %param.25) | data formatting | bytes 18874368 | tf_op args[5]
  38.4 12.6 %copy.27 = bf16[1,1536,3072]{1,2,0:T(8,128)(2,1)} copy(bf16[1,1536,3072]{2,1,0:T(8,128)(2,1)} %param.26) | data formatting | bytes 18874368 | tf_op args[6]
  51.2 7.4 %all-to-all-start = ((bf16[16,64,192]{2,1,0:T(8,128)(2,1)}), bf16[16,64,192]{2,1,0:T(8,128)(2,1)}, u32[]{:S(2)}, u32[]{:S(2)}) async-start(bf16[16,64,192]{2,1,0:T(8,128)(2,1)} %get-tuple-element.213), calls=%async_computation | async-start | bytes 1048576 | tf_op jit(solution)/shard_map/all_to_all | solution.py:139
  58.7 0.6 copy.29
  59.6 0.4 fusion.41
  60.0 9.6 %all-to-all-done = bf16[16,64,192]{2,1,0:T(8,128)(2,1)} async-done(((bf16[16,64,192]{2,1,0:T(8,128)(2,1)}), bf16[16,64,192]{2,1,0:T(8,128)(2,1)}, u32[]{:S(2)}, u32[]{:S(2)}) %all-to-all-start) | async-done | bytes 393248 | tf_op jit(solution)/shard_map/all_to_all | solution.py:139
  69.5 4.2 all-to-all-start.2
  74.0 1.1 convert_bitcast_fusion.1
  75.1 1.6 copy.24
  76.7 1.4 reshape.156
  78.6 1.2 multiply_subtract_fusion
  79.8 1.2 subtract_convert_fusion
  81.0 1.6 maximum_convert_fusion
  82.6 40.6 %while.18 = (s32[]{:T(128)}, f32[32,64]{1,0:T(8,128)S(1)}, f32[32,64]{1,0:T(8,128)S(1)}, f32[64,32,96]{2,0,1:T(8,128)}, s32[]{:T(128)}, /*index=5*/bf16[1536,307...) while((s32[]{:T(128)}, f32[32,64]{1,0:T(8,128)S(1)}, ...), condition=%wide.region_5.7_spmd.clone, body=%wide.region_2.6_spmd.clone.sunk | while | flops 414790656 | bytes 51906808 | solution.py:94
  82.6 0.7 add_compare_fusion.2
  83.3 3.3 constant_dynamic-slice_fusion.3
  86.7 2.8 bitcast_reduce_fusion.2
  89.5 3.4 fusion.84
  92.9 2.6 fusion.86
  95.5 0.7 add_compare_fusion.2
  96.2 3.3 constant_dynamic-slice_fusion.3
  99.5 2.8 bitcast_reduce_fusion.2
  102.3 3.4 fusion.84
  105.8 3.6 fusion.86
  109.3 0.7 add_compare_fusion.2
  110.0 3.3 constant_dynamic-slice_fusion.3
  113.4 2.8 bitcast_reduce_fusion.2
  116.2 3.4 fusion.84
  119.6 3.6 fusion.86
  123.2 1.4 copy.33
  124.9 1.6 fusion.44
  126.9 1.2 fusion.24
  128.4 1.5 convert_element_type.94
  130.0 0.7 all-gather.13.cloned.1.call-update
  131.0 1.2 sort.17
  132.4 60.7 %all-gather.7.cloned.1.call-done = bf16[1024,3072]{1,0:T(8,128)(2,1)} async-done(((bf16[64,3072]{1,0:T(8,128)(2,1)}), bf16[1024,3072]{1,0:T(8,128)(2,1)}) %all-gather.7.cloned.1.call-update) | async-done | bytes 6291472 | tf_op jit(solution)/shard_map/all_gather | solution.py:156
  193.1 4.9 %fusion.45 = f32[1024,192]{1,0:T(8,128)S(1)} fusion(bf16[1024,3072]{1,0:T(8,128)(2,1)} %all-gather.7.cloned.1.call-done, bf16[3072,192]{0,1:T(8,128)(2,1)} %all-gather.9.cloned.1.call-done), kind=kOutput, calls=%fused_computation.98 | convolution fusion | flops 1207959552 | bytes 8257536 | tf_op jit(solution)/shard_map/dot_general | solution.py:155
  198.1 0.6 gather_fusion
  199.3 38.4 %psum.7 = f32[1024]{0:T(1024)S(1)} all-reduce(f32[1024]{0:T(1024)S(1)} %fusion.27), channel_id=1, replica_groups=mesh['row'=8,'col'=16] {'col'}, use_global_device_ids=true, to_apply=%region_9.11 | all-reduce | flops 1024 | bytes 8192 | tf_op jit(solution)/shard_map/psum | solution.py:168
  237.7 0.9 fusion.29
  238.6 0.5 all-gather.17.cloned.1.call-update
  239.2 0.5 all-gather.15.cloned.1.call-update
  239.8 56.6 %all-gather.11.cloned.1.call-done = bf16[1024,3072]{0,1:T(8,128)(2,1)} async-done(((bf16[1024,192]{0,1:T(8,128)(2,1)}), bf16[1024,3072]{0,1:T(8,128)(2,1)}) %all-gather.11.cloned.1.call-update) | async-done | bytes 6291472 | tf_op jit(solution)/shard_map/all_gather | solution.py:171
  296.4 6.5 %fusion.46 = f32[1024,512]{1,0:T(8,128)S(1)} fusion(bf16[1024,3072]{0,1:T(8,128)(2,1)} %all-gather.11.cloned.1.call-done, bf16[3072,512]{1,0:T(8,128)(2,1)} %all-gather.13.cloned.1.call-done), kind=kOutput, calls=%fused_computation.99 | convolution fusion | flops 3221225472 | bytes 11534336 | tf_op jit(solution)/shard_map/dot_general | solution.py:172
  302.9 22.3 %all-gather.17.cloned.1.call-done = bf16[512,3072]{1,0:T(8,128)(2,1)} async-done(((bf16[512,384]{1,0:T(8,128)(2,1)}), bf16[512,3072]{1,0:T(8,128)(2,1)}) %all-gather.17.cloned.1.call-update) | async-done | bytes 3145744 | tf_op jit(solution)/shard_map/all_gather | solution.py:185
  325.2 29.4 %all-gather.15.cloned.1.call-done = bf16[3072,512]{1,0:T(8,128)(2,1)} async-done(((bf16[384,512]{1,0:T(8,128)(2,1)}), bf16[3072,512]{1,0:T(8,128)(2,1)}) %all-gather.15.cloned.1.call-update) | async-done | bytes 3145744 | tf_op jit(solution)/shard_map/all_gather | solution.py:179
  354.6 12.8 %convolution_convert_fusion = bf16[1024,3072]{0,1:T(8,128)(2,1)} fusion(bf16[512,3072]{1,0:T(8,128)(2,1)} %all-gather.17.cloned.1.call-done, f32[1024,512]{1,0:T(8,128)S(1)} %fusion.46, bf16[1024,3072]{0,1:T(8,128)(2,1)} %all-gather.11.cloned.1.call-done, bf16[3072,512]{1,0:T(8,128)(2,1)} %all-gather.15.cloned.1.call-done), kind=kOutput, calls=%fused_computation.28 | convolution fusion | flops 6448742400 | bytes 20971520 | tf_op jit(solution)/shard_map/dot_general | solution.py:183
  367.5 1.0 copy-done.2
  368.9 0.5 all_to_all.32
  369.4 0.7 convert_element_type.103
  370.1 0.8 fusion.19
  371.0 0.8 fusion.20
  371.8 77.5 %reduce-scatter.2.cloned.1.call-done = bf16[1024,192]{0,1:T(8,128)(2,1)} async-done(((bf16[1024,3072]{0,1:T(8,128)(2,1)}), bf16[1024,192]{0,1:T(8,128)(2,1)}) %reduce-scatter.2.cloned.1.call-update) | async-done | bytes 393232 | tf_op jit(solution)/shard_map/reduce_scatter | solution.py:188
  449.3 1.9 fusion.30
  (86 shorter events, 5.2 us)
Async XLA Ops:
  7.2 5.0 %copy-start.3 = (bf16[1024,192]{0,1:T(8,128)(2,1)S(1)}, bf16[1024,192]{0,1:T(8,128)(2,1)}, u32[]{:S(2)}) copy-start(bf16[1024,192]{0,1:T(8,128)(2,1)} %param.22) | copy-start | bytes 1179652
  11.0 12.1 %copy-start.6 = (s32[1,64]{1,0:T(1,128)S(1)}, s32[1,64]{1,0:T(1,128)}, u32[]{:S(2)}) copy-start(s32[1,64]{1,0:T(1,128)} %param.28) | copy-start | bytes 772
  14.3 36.9 %all-to-all-start.1 = ((bf16[16,64,192]{2,1,0:T(8,128)(2,1)}), bf16[16,64,192]{2,1,0:T(8,128)(2,1)S(1)}, u32[]{:S(2)}, u32[]{:S(2)}) async-start(bf16[16,64,192]{2,1,0:T(8,128)(2,1)} %get-tuple-element.212), calls=%async_computation.1 | async-start | bytes 1048576 | tf_op jit(solution)/shard_map/all_to_all | solution.py:140
  22.3 110.1 %all-gather.9.cloned.1.call-start = ((), (), s32[]{:S(2)}) async-start(), calls=%async_computation.5 | async-start | bytes 1327104 | tf_op jit(solution)/shard_map/all_gather | solution.py:154
  51.2 18.3 %all-to-all-start = ((bf16[16,64,192]{2,1,0:T(8,128)(2,1)}), bf16[16,64,192]{2,1,0:T(8,128)(2,1)}, u32[]{:S(2)}, u32[]{:S(2)}) async-start(bf16[16,64,192]{2,1,0:T(8,128)(2,1)} %get-tuple-element.213), calls=%async_computation | async-start | bytes 1048576 | tf_op jit(solution)/shard_map/all_to_all | solution.py:139
  69.5 53.7 %all-to-all-start.2 = ((bf16[16,64,192]{2,1,0:T(8,128)(2,1)}), bf16[16,64,192]{2,1,0:T(8,128)(2,1)}, u32[]{:S(2)}, u32[]{:S(2)}) async-start(bf16[16,64,192]{2,1,0:T(8,128)(2,1)} %get-tuple-element.211), calls=%async_computation.2 | async-start | bytes 1048576 | tf_op jit(solution)/shard_map/all_to_all | solution.py:141
  73.8 119.4 %all-gather.7.cloned.1.call-start = ((), (), s32[]{:S(2)}) async-start(), calls=%async_computation.4 | async-start | bytes 6684672 | tf_op jit(solution)/shard_map/all_gather | solution.py:156
  83.3 3.3 copy-start.1
  89.5 3.4 copy-start
  96.2 3.3 copy-start.1
  102.3 3.4 copy-start
  110.0 3.3 copy-start.1
  116.2 3.4 copy-start
  123.2 3.6 copy-start.9
  126.8 4.2 copy-start.7
  126.8 5.6 %copy-start.8 = (bf16[192]{0:T(256)(128)(2,1)S(1)}, bf16[192]{0:T(256)(128)(2,1)}, u32[]{:S(2)}) copy-start(bf16[192]{0:T(256)(128)(2,1)} %param.32) | copy-start | bytes 1156
  129.9 109.9 %all-gather.13.cloned.1.call-start = ((), (), s32[]{:S(2)}) async-start(), calls=%async_computation.7 | async-start | bytes 3538944 | tf_op jit(solution)/shard_map/all_gather | solution.py:174
  130.7 165.7 %all-gather.11.cloned.1.call-start = ((), (), s32[]{:S(2)}) async-start(), calls=%async_computation.6 | async-start | bytes 6684672 | tf_op jit(solution)/shard_map/all_gather | solution.py:171
  198.0 1.0 copy-start.4
  238.6 86.7 %all-gather.17.cloned.1.call-start = ((), (), s32[]{:S(2)}) async-start(), calls=%async_computation.9 | async-start | bytes 3538944 | tf_op jit(solution)/shard_map/all_gather | solution.py:185
  239.2 115.5 %all-gather.15.cloned.1.call-start = ((), (), s32[]{:S(2)}) async-start(), calls=%async_computation.8 | async-start | bytes 3538944 | tf_op jit(solution)/shard_map/all_gather | solution.py:179
  239.8 209.5 %reduce-scatter.2.cloned.1.call-start = ((), (), s32[]{:S(2)}) async-start(), calls=%async_computation.10 | async-start | bytes 6684672 | tf_op jit(solution)/shard_map/reduce_scatter | solution.py:188
  367.5 1.0 copy-start.2
  367.5 2.7 copy-start.5
Sparse Core Ops, SparseCore 0:
  24.8 25.2 all-gather.8
  130.1 63.0 all-gather.6
  194.8 27.2 all-gather.12
  238.7 57.6 all-gather.10
  298.0 27.2 all-gather.16
  326.8 27.8 all-gather.14
  367.6 81.6 reduce-scatter.1
where the time goes:
time: 459 us; the launch traced here: 458 us
  waiting for transfers between devices  259 us (56%)
  local copies, waits for them, and re-layouts  51.6 us (11%)
  matrix products  48 us (10%)
  blocking collectives  38.4 us (8%)
  other arithmetic  25 us (5%)
  starting transfers between devices  20.3 us (4%)
  between operations  15.9 us (3%)
    reduce_scatter x1, waiting for transfers between devices, body(): lax.psum_scatter(partial_terms.astype(jnp.bfloat16), 'col', scatter_dimen...  77.5 us
    all_gather x1, waiting for transfers between devices, body(): lax.all_gather(attended, 'col', axis=0, tiled=True)  60.7 us
    all_gather x1, waiting for transfers between devices, body(): gathered = lax.all_gather(normed, 'col', axis=1, tiled=True)  56.6 us
    psum x1, blocking collectives, body(): row_totals = lax.psum(local_sums, 'col')  38.4 us
    all_gather x1, waiting for transfers between devices, body(): lax.all_gather(up_weight, 'row', axis=0, tiled=True)  29.4 us
    unnamed x21, local copies, waits for them, and re-layouts  29 us
    all_gather x1, waiting for transfers between devices, body(): lax.all_gather(down_weight, 'row', axis=1, tiled=True)  22.3 us
    dot_general x1, matrix products, body(): jnp.dot(hidden, lax.all_gather(down_weight, 'row', axis=1, tiled=True), p...  12.8 us
  transfers between devices with their start and end apart: 10, of which 6 were waited for; matrix products, arithmetic and copies ran while one was open for 22% of the time, Pallas kernels for 0%

commit v1 on v0

--- a/solution.py
+++ b/solution.py
@@ -3,11 +3,14 @@
 import jax
 import jax.numpy as jnp
 from jax import lax
+from jax.experimental import pallas as pl
+from jax.experimental.pallas import tpu as pltpu
 from jax.sharding import PartitionSpec as P
 
 D = 3072
 HEADS = 32
 HEAD_DIM = 96
+MESH = pl.DeviceIdType.MESH
 
 
 def ancestry(parent_row):
@@ -106,6 +109,298 @@
         jnp.bfloat16
     )
     return (attended, new_keys, new_values)
+
+
+def mlp_kernel(
+    st_hbm, w_hbm, dn_hbm, gain_ref, out_ref,
+    S, W, DN, acc, H, ss, T, R, Q, T2, R2,
+    loc_sem, ag_send, ag_recv, rs_send, rs_recv, rt_send, rt_recv,
+):
+    me = lax.axis_index("col")
+    z, x = me // 4, me % 4
+    halves = (0, 1)
+    a_own, b_own = (x, z), (z, x)
+
+    def blk(h, a, b):
+        return b * 4 + a if h == 0 else a * 4 + b
+
+    def peer1(h, d):
+        return blk(h, (a_own[h] + d + 4) % 4, b_own[h])
+
+    def peer2(h, d):
+        return blk(h, a_own[h], (b_own[h] + d + 4) % 4)
+
+    stream_in = [
+        pltpu.make_async_copy(st_hbm.at[:, pl.ds(512 * h, 512)], S.at[h, me], loc_sem.at[h])
+        for h in halves
+    ]
+    w_in = pltpu.make_async_copy(w_hbm, W, loc_sem.at[2])
+    dn_in = pltpu.make_async_copy(dn_hbm, DN, loc_sem.at[3])
+    for c in stream_in:
+        c.start()
+    w_in.start()
+    dn_in.start()
+
+    barrier = pltpu.get_barrier_semaphore()
+    for p in (peer1(0, 1), peer1(0, -1), peer1(1, 1), peer1(1, -1)):
+        pl.semaphore_signal(barrier, inc=1, device_id={"col": p}, device_id_type=MESH)
+    pl.semaphore_wait(barrier, 4)
+    for c in stream_in:
+        c.wait()
+
+    sent = []
+
+    def push(h, k, c, target, rows=None):
+        ref = S.at[h, c] if rows is None else S.at[h, c, pl.ds(rows, 96)]
+        cp = pltpu.make_async_remote_copy(
+            src_ref=ref, dst_ref=ref, send_sem=ag_send.at[h, k], recv_sem=ag_recv.at[h, k],
+            device_id={"col": target}, device_id_type=MESH,
+        )
+        cp.start()
+        sent.append(cp)
+
+    def arrived(h, k, c, rows=None):
+        ref = S.at[h, c] if rows is None else S.at[h, c, pl.ds(rows, 96)]
+        pltpu.make_async_remote_copy(
+            src_ref=ref, dst_ref=ref, send_sem=ag_send.at[h, k], recv_sem=ag_recv.at[h, k],
+            device_id={"col": me}, device_id_type=MESH,
+        ).wait_recv()
+
+    def at(h, da, db):
+        return blk(h, (a_own[h] + da + 4) % 4, (b_own[h] + db + 4) % 4)
+
+    offs = (0, -1, 1, 2)
+    for h in halves:
+        push(h, 0, me, peer1(h, 1))
+        push(h, 1, me, peer1(h, -1))
+    for h in halves:
+        push(h, 4, me, peer2(h, 1))
+        push(h, 5, me, peer2(h, -1))
+
+    acc[...] = jnp.zeros_like(acc)
+    ss[...] = jnp.zeros_like(ss)
+    w_in.wait()
+
+    @pl.loop(0, 8)
+    def _(r):
+        W[r] = W[r] * gain_ref[r]
+
+    for h in halves:
+        arrived(h, 0, at(h, -1, 0))
+        push(h, 2, at(h, -1, 0), peer1(h, 1), 0)
+        push(h, 8, at(h, -1, 0), peer2(h, 1))
+        push(h, 9, at(h, -1, 0), peer2(h, -1))
+        arrived(h, 1, at(h, 1, 0))
+        push(h, 3, at(h, 1, 0), peer1(h, -1), 96)
+        push(h, 12, at(h, 1, 0), peer2(h, 1))
+        push(h, 13, at(h, 1, 0), peer2(h, -1))
+
+    def second(j):
+        for h in halves:
+            base = 4 + 4 * j
+            arrived(h, base, at(h, offs[j], -1))
+            push(h, base + 2, at(h, offs[j], -1), peer2(h, 1), 0)
+            arrived(h, base + 1, at(h, offs[j], 1))
+            push(h, base + 3, at(h, offs[j], 1), peer2(h, -1), 96)
+
+    def square(h, c):
+        v = S[h, c].astype(jnp.float32)
+        ss[h] += jnp.sum(v * v, axis=0, keepdims=True)
+
+    def fold_a(zz):
+        for i in range(4):
+            square(0, zz * 4 + i)
+        k0 = S[0, pl.ds(zz * 4, 2)].reshape(384, 512)
+        k1 = S[0, pl.ds(zz * 4 + 2, 2)].reshape(384, 512)
+
+        @pl.loop(0, 4)
+        def _(m):
+            rows = pl.ds(pl.multiple_of(m * 256, 256), 256)
+            acc[0, rows] += jnp.dot(
+                W[2 * zz, rows], k0, preferred_element_type=jnp.float32
+            ) + jnp.dot(W[2 * zz + 1, rows], k1, preferred_element_type=jnp.float32)
+
+    def fold_b(q):
+        @pl.loop(0, 2)
+        def _(g):
+            for i in range(2):
+                for e in range(2):
+                    square(1, (2 * g + i) * 4 + 2 * q + e)
+            k0 = S[1, pl.ds(8 * g + 2 * q, 2)].reshape(384, 512)
+            k1 = S[1, pl.ds(8 * g + 4 + 2 * q, 2)].reshape(384, 512)
+
+            @pl.loop(0, 4)
+            def _(m):
+                rows = pl.ds(pl.multiple_of(m * 256, 256), 256)
+                acc[1, rows] += jnp.dot(
+                    W[4 * g + q, rows], k0, preferred_element_type=jnp.float32
+                ) + jnp.dot(W[4 * g + 2 + q, rows], k1, preferred_element_type=jnp.float32)
+
+    second(0)
+    for h in halves:
+        arrived(h, 2, at(h, 2, 0), 0)
+        arrived(h, 3, at(h, 2, 0), 96)
+        push(h, 16, at(h, 2, 0), peer2(h, 1))
+        push(h, 17, at(h, 2, 0), peer2(h, -1))
+    fold_a(z)
+    second(1)
+    second(2)
+    second(3)
+
+    @pl.loop(0, 2)
+    def _(i):
+        fold_a((z + 3 + 2 * i) % 4)
+
+    fold_b(x // 2)
+    for h in halves:
+        for j in range(4):
+            arrived(h, 6 + 4 * j, at(h, offs[j], 2), 0)
+            arrived(h, 7 + 4 * j, at(h, offs[j], 2), 96)
+    fold_a((z + 2) % 4)
+    fold_b(1 - x // 2)
+    for cp in sent:
+        cp.wait_send()
+
+    for h in halves:
+        factor = lax.rsqrt(ss[h] * (1.0 / D) + 1e-05)
+
+        @pl.loop(0, 4)
+        def _(m, h=h, factor=factor):
+            rows = pl.ds(pl.multiple_of(m * 128, 128), 128)
+            uprows = pl.ds(pl.multiple_of(512 + m * 128, 128), 128)
+            g = acc[h, rows] * factor
+            u = acc[h, uprows] * factor
+            H[h, rows] = (g / (1.0 + jnp.exp(-g)) * u).astype(jnp.bfloat16)
+
+    dn_in.wait()
+
+    def part(h, c):
+        rows = pl.ds(pl.multiple_of(c * 192, 192), 192)
+        return jnp.dot(DN[rows], H[h], preferred_element_type=jnp.float32)
+
+    sent = []
+
+    def send1(h, kind, i):
+        d = 1 if kind % 2 == 0 else -1
+        cp = pltpu.make_async_remote_copy(
+            src_ref=T.at[h, kind, i], dst_ref=R.at[h, kind, i],
+            send_sem=rs_send.at[h, kind, i], recv_sem=rs_recv.at[h, kind, i],
+            device_id={"col": peer1(h, d)}, device_id_type=MESH,
+        )
+        cp.start()
+        sent.append(cp)
+
+    def got1(h, kind, i):
+        pltpu.make_async_remote_copy(
+            src_ref=T.at[h, kind, i], dst_ref=R.at[h, kind, i],
+            send_sem=rs_send.at[h, kind, i], recv_sem=rs_recv.at[h, kind, i],
+            device_id={"col": me}, device_id_type=MESH,
+        ).wait_recv()
+
+    def dest(h, da, b):
+        return blk(h, (a_own[h] + da + 4) % 4, b)
+
+    for kind, da, b0 in ((0, 2, 0), (1, 2, 2), (4, 1, 2), (5, -1, 0)):
+        for i in range(2):
+            for h in halves:
+                T[h, kind, i] = part(h, dest(h, da, b0 + i)).astype(jnp.bfloat16)
+                send1(h, kind, i)
+    for kind, da, b0 in ((2, 1, 0), (3, -1, 2)):
+        for i in range(2):
+            for h in halves:
+                mine = part(h, dest(h, da, b0 + i))
+                got1(h, kind - 2, i)
+                T[h, kind, i] = (mine + R[h, kind - 2, i].astype(jnp.float32)).astype(jnp.bfloat16)
+                send1(h, kind, i)
+    for b in range(4):
+        for h in halves:
+            mine = part(h, dest(h, 0, b))
+            s_kind, d_kind = (2, 5) if b < 2 else (3, 4)
+            got1(h, s_kind, b % 2)
+            got1(h, d_kind, b % 2)
+            Q[h, b] = (
+                mine
+                + R[h, s_kind, b % 2].astype(jnp.float32)
+                + R[h, d_kind, b % 2].astype(jnp.float32)
+            ).astype(jnp.bfloat16)
+    for h in halves:
+        for i in range(2):
+            pass
+
+    def copy2(h, kind, src, target):
+        return pltpu.make_async_remote_copy(
+            src_ref=src, dst_ref=R2.at[h, kind],
+            send_sem=rt_send.at[h, kind], recv_sem=rt_recv.at[h, kind],
+            device_id={"col": target}, device_id_type=MESH,
+        )
+
+    def bmod(h, d):
+        return (b_own[h] + d + 4) % 4
+
+    for h in halves:
+        for kind, d, row in ((0, 2, 0), (1, 2, 96), (4, 1, 96), (5, -1, 0)):
+            cp = copy2(h, kind, Q.at[h, bmod(h, d), pl.ds(row, 96)], peer2(h, 1 if kind % 2 == 0 else -1))
+            cp.start()
+            sent.append(cp)
+    for h in halves:
+        for kind, d, row in ((2, 1, 0), (3, -1, 96)):
+            copy2(h, kind - 2, T2.at[h, 0], me).wait_recv()
+            T2[h, kind - 2] = (
+                Q[h, bmod(h, d), pl.ds(row, 96)].astype(jnp.float32)
+                + R2[h, kind - 2].astype(jnp.float32)
+            ).astype(jnp.bfloat16)
+            cp = copy2(h, kind, T2.at[h, kind - 2], peer2(h, 1 if kind == 2 else -1))
+            cp.start()
+            sent.append(cp)
+    for h in halves:
+        for row, s_kind, d_kind in ((0, 2, 5), (96, 3, 4)):
+            copy2(h, s_kind, T2.at[h, 0], me).wait_recv()
+            copy2(h, d_kind, T2.at[h, 0], me).wait_recv()
+            out_ref[pl.ds(row, 96), pl.ds(512 * h, 512)] = (
+                S[h, me, pl.ds(row, 96)].astype(jnp.float32)
+                + Q[h, b_own[h], pl.ds(row, 96)].astype(jnp.float32)
+                + R2[h, s_kind].astype(jnp.float32)
+                + R2[h, d_kind].astype(jnp.float32)
+            ).astype(jnp.bfloat16)
+    for cp in sent:
+        cp.wait_send()
+
+
+def mlp_call(stream_t, weights, down_t, gain):
+    anyspace = pl.BlockSpec(memory_space=pl.ANY)
+    vmem = pl.BlockSpec(memory_space=pltpu.VMEM)
+    bf, f32 = jnp.bfloat16, jnp.float32
+    dma = pltpu.SemaphoreType.DMA
+    return pl.pallas_call(
+        mlp_kernel,
+        out_shape=jax.ShapeDtypeStruct((192, 1024), bf),
+        in_specs=[anyspace, anyspace, anyspace, vmem],
+        out_specs=vmem,
+        scratch_shapes=[
+            pltpu.VMEM((2, 16, 192, 512), bf),
+            pltpu.VMEM((8, 1024, 384), bf),
+            pltpu.VMEM((3072, 512), bf),
+            pltpu.VMEM((2, 1024, 512), f32),
+            pltpu.VMEM((2, 512, 512), bf),
+            pltpu.VMEM((2, 1, 512), f32),
+            pltpu.VMEM((2, 6, 2, 192, 512), bf),
+            pltpu.VMEM((2, 6, 2, 192, 512), bf),
+            pltpu.VMEM((2, 4, 192, 512), bf),
+            pltpu.VMEM((2, 2, 96, 512), bf),
+            pltpu.VMEM((2, 6, 96, 512), bf),
+            dma((4,)),
+            dma((2, 20)),
+            dma((2, 20)),
+            dma((2, 6, 2)),
+            dma((2, 6, 2)),
+            dma((2, 6)),
+            dma((2, 6)),
+        ],
+        compiler_params=pltpu.CompilerParams(
+            collective_id=0, has_side_effects=True, vmem_limit_bytes=60 * 1024 * 1024
+        ),
+        name="mlp",
+    )(stream_t, weights, down_t, gain)
 
 
 def body(
@@ -151,44 +446,25 @@
         draft_counts[0],
         accepted[0],
     )
-    weight_cols = lax.all_gather(out_weight, "row", axis=0, tiled=True)
-    projected = jnp.dot(
-        lax.all_gather(attended, "col", axis=0, tiled=True),
-        weight_cols,
+    wo_t = lax.all_gather(out_weight.T[None], "row", axis=0, tiled=True)
+    gate_up = lax.all_gather(
+        jnp.concatenate([gate_weight.T, up_weight.T], axis=0)[None], "row", axis=0, tiled=True
+    )
+    down_t = lax.all_gather(down_weight.T, "row", axis=0, tiled=True)
+    gain = lax.all_gather(norm_gain, "col", axis=0, tiled=True).reshape(8, 1, 384)
+    every = lax.all_gather(attended, "col", axis=0, tiled=True)
+    projected = lax.dot_general(
+        jnp.transpose(wo_t, (1, 0, 2)).reshape(192, 3072),
+        every,
+        (((1,), (1,)), ((), ())),
         preferred_element_type=jnp.float32,
     )
+    stream_t = (to_slots(residual).T.astype(jnp.float32) + projected).astype(jnp.bfloat16)
+    out_t = mlp_call(stream_t, gate_up, down_t, gain)
     inverse = jnp.argsort(dealt_order)
-    projected = jnp.take(
-        projected.reshape(columns, draft_rows, projected.shape[1]), inverse, axis=0
-    ).reshape(rows_here, projected.shape[1])
-    stream_full = residual.astype(jnp.float32) + projected
-    stream = stream_full.astype(jnp.bfloat16)
-    stream_wide = lax.optimization_barrier(stream).astype(jnp.float32)
-    local_sums = jnp.sum(stream_wide * stream_wide, axis=1)
-    row_totals = lax.psum(local_sums, "col")
-    factor = lax.rsqrt(row_totals / D + 1e-05)[:, None]
-    normed = (stream_wide * factor * norm_gain.astype(jnp.float32)[None, :]).astype(jnp.bfloat16)
-    gathered = lax.all_gather(normed, "col", axis=1, tiled=True)
-    gate_next = jnp.dot(
-        gathered,
-        lax.all_gather(gate_weight, "row", axis=0, tiled=True),
-        preferred_element_type=jnp.float32,
-    )
-    up_next = jnp.dot(
-        gathered,
-        lax.all_gather(up_weight, "row", axis=0, tiled=True),
-        preferred_element_type=jnp.float32,
-    )
-    hidden = (jax.nn.silu(gate_next) * up_next).astype(jnp.bfloat16)
-    partial_terms = jnp.dot(
-        hidden,
-        lax.all_gather(down_weight, "row", axis=1, tiled=True),
-        preferred_element_type=jnp.float32,
-    )
-    summed = lax.psum_scatter(
-        partial_terms.astype(jnp.bfloat16), "col", scatter_dimension=1, tiled=True
-    ).astype(jnp.float32)
-    layer_out = (stream_wide + summed).astype(jnp.bfloat16)
+    layer_out = jnp.take(out_t.T.reshape(columns, draft_rows, 192), inverse, axis=0).reshape(
+        rows_here, 192
+    )
     return (layer_out, new_keys[None], new_values[None])
 
 

time: 459 us -> 321 us (0.70)
  waiting for transfers between devices: 259 us -> 41.4 us
  Pallas kernels: 0 us -> 86.1 us
  matrix products: 48 us -> 30.4 us
  local copies, waits for them, and re-layouts: 51.6 us -> 64.4 us
    all_gather x6 -> x4, waiting for transfers between devices: 169 us -> 25.8 us  [the longest x1 23 us: body(): down_t = lax.all_gather(down_weight.T, 'row', axis=0, tiled=True)]
    pallas_call x0 -> x1, Pallas kernels: none -> 86.1 us  [mlp_call(): pl.pallas_call(mlp_kernel, out_shape=jax.ShapeDtypeStruct((192, 1024), bf...]
    reduce_scatter x1 -> x0, waiting for transfers between devices: 77.5 us -> none  [body(): lax.psum_scatter(partial_terms.astype(jnp.bfloat16), 'col', scatter_dimen...]
    psum x1 -> x0, blocking collectives: 38.4 us -> none  [body(): row_totals = lax.psum(local_sums, 'col')]
    unnamed x0 -> x1, blocking collectives: none -> 37.9 us
    dot_general x3 -> x1, matrix products: 24.2 us -> 5.75 us  [body(): lax.dot_general(jnp.transpose(wo_t, (1, 0, 2)).reshape(192, 3072), every,...]
    all_to_all x1, waiting for transfers between devices: 9.56 us -> 0.01 us  [body(): lax.all_to_all(to_slots(queries), 'col', split_axis=0, concat_axis=1, til...]
    all_gather x0 -> x1, local copies, waits for them, and re-layouts: none -> 8.68 us  [body(): lax.all_gather(jnp.concatenate([gate_weight.T, up_weight.T], axis=0)[None...]
  transfers between devices with their start and end apart: 10 -> 7, of which waited for: 6 -> 4; matrix products, arithmetic and copies ran while one was open for 22% -> 36% of each run, Pallas kernels for 0% -> 0%
where the time goes in v1:
time: 321 us; the launch traced here: 319 us
  Pallas kernels  86.1 us (27%)
  local copies, waits for them, and re-layouts  64.4 us (20%)
  waiting for transfers between devices  41.4 us (13%)
  blocking collectives  37.9 us (12%)
  matrix products  30.4 us (9%)
  other arithmetic  22.8 us (7%)
  starting transfers between devices  19.3 us (6%)
  between operations  16.3 us (5%)
    pallas_call x1, Pallas kernels, mlp_call(): pl.pallas_call(mlp_kernel, out_shape=jax.ShapeDtypeStruct((192, 1024), bf...  86.1 us
    unnamed x1, blocking collectives  37.9 us
    unnamed x42, local copies, waits for them, and re-layouts  32.5 us
    all_gather x1, waiting for transfers between devices, body(): down_t = lax.all_gather(down_weight.T, 'row', axis=0, tiled=True)  23 us
    dot_general x4, matrix products, fold_block(): jnp.einsum('hqk,khd->qhd', weights.astype(jnp.bfloat16), value_heads, pre...  12.2 us
    reduce_sum x4, other arithmetic, fold_block(): row_totals = row_totals * rescale + jnp.sum(weights, axis=2)  11.6 us
    dynamic_slice x3, local copies, waits for them, and re-layouts, cache_step(): value_block = lax.dynamic_slice_in_dim(cache_v, block_start, block_rows, 0)  9.96 us
    dot_general x4, matrix products, fold_block(): jnp.einsum('qhd,khd->hqk', q_heads, key_heads, preferred_element_type=jnp...  9.63 us
  transfers between devices with their start and end apart: 7, of which 4 were waited for; matrix products, arithmetic and copies ran while one was open for 36% of the time, Pallas kernels for 0%

profile of v1, /device:TPU:0, one launch (start us, length us, event | category | flops | bytes accessed | tf_op | source)
XLA Modules:
  0.0 318.8 jit_solution(11881843753745164301)
XLA Ops:
  7.2 0.7 all-gather.11.cloned.1.call-update
  7.9 1.2 copy.35
  9.1 1.2 copy.26
  10.3 0.7 compare_select_fusion.1
  11.0 0.6 gather_fusion.3
  11.6 0.6 gather_fusion.1
  12.4 0.6 gather_fusion.2
  13.2 0.6 gather_fusion
  13.8 1.4 broadcast_select_fusion.1
  15.3 8.0 %all-to-all-start.1 = ((bf16[16,64,192]{2,1,0:T(8,128)(2,1)}), bf16[16,64,192]{2,1,0:T(8,128)(2,1)S(1)}, u32[]{:S(2)}, u32[]{:S(2)}) async-start(bf16[16,64,192]{2,1,0:T(8,128)(2,1)} %get-tuple-element.216), calls=%async_computation.1 | async-start | bytes 1048576 | tf_op jit(solution)/shard_map/all_to_all | solution.py:435
  23.3 2.0 pad_maximum_fusion
  27.9 6.9 %all-to-all-done.1 = bf16[16,64,192]{2,1,0:T(8,128)(2,1)S(1)} async-done(((bf16[16,64,192]{2,1,0:T(8,128)(2,1)}), bf16[16,64,192]{2,1,0:T(8,128)(2,1)S(1)}, u32[]{:S(2)}, u32[]{:S(2)}) %all-to-all-start.1) | async-done | bytes 393248 | tf_op jit(solution)/shard_map/all_to_all | solution.py:435
  34.8 3.6 %all-to-all-start = ((bf16[16,64,192]{2,1,0:T(8,128)(2,1)}), bf16[16,64,192]{2,1,0:T(8,128)(2,1)S(1)}, u32[]{:S(2)}, u32[]{:S(2)}) async-start(bf16[16,64,192]{2,1,0:T(8,128)(2,1)} %get-tuple-element.215), calls=%async_computation | async-start | bytes 1048576 | tf_op jit(solution)/shard_map/all_to_all | solution.py:434
  38.4 12.8 %copy.25 = bf16[1,1536,3072]{1,2,0:T(8,128)(2,1)} copy(bf16[1,1536,3072]{2,1,0:T(8,128)(2,1)} %param.25) | data formatting | bytes 18874368 | tf_op args[5]
  51.2 12.6 %copy.30 = bf16[1,1536,3072]{1,2,0:T(8,128)(2,1)} copy(bf16[1,1536,3072]{2,1,0:T(8,128)(2,1)} %param.26) | data formatting | bytes 18874368 | tf_op args[6]
  64.1 7.2 %all-to-all-start.2 = ((bf16[16,64,192]{2,1,0:T(8,128)(2,1)}), bf16[16,64,192]{2,1,0:T(8,128)(2,1)}, u32[]{:S(2)}, u32[]{:S(2)}) async-start(bf16[16,64,192]{2,1,0:T(8,128)(2,1)} %get-tuple-element.214), calls=%async_computation.2 | async-start | bytes 1048576 | tf_op jit(solution)/shard_map/all_to_all | solution.py:436
  71.6 0.6 copy.32
  72.6 0.6 copy.27
  73.4 8.0 %all-to-all-done.2 = bf16[16,64,192]{2,1,0:T(8,128)(2,1)} async-done(((bf16[16,64,192]{2,1,0:T(8,128)(2,1)}), bf16[16,64,192]{2,1,0:T(8,128)(2,1)}, u32[]{:S(2)}, u32[]{:S(2)}) %all-to-all-start.2) | async-done | bytes 393248 | tf_op jit(solution)/shard_map/all_to_all | solution.py:436
  81.4 1.3 copy.36
  82.8 1.1 reshape.160
  83.8 0.4 fusion.38
  84.2 0.4 fusion.39
  84.6 1.2 multiply_subtract_fusion
  85.8 1.2 subtract_convert_fusion
  87.1 0.6 maximum_convert_fusion
  87.7 1.4 fusion.41
  89.1 40.2 %while.18 = (s32[]{:T(128)}, f32[32,64]{1,0:T(8,128)S(1)}, f32[32,64]{1,0:T(8,128)S(1)}, f32[64,32,96]{2,0,1:T(8,128)}, s32[]{:T(128)}, /*index=5*/bf16[1536,307...) while((s32[]{:T(128)}, f32[32,64]{1,0:T(8,128)S(1)}, ...), condition=%wide.region_4.6_spmd.clone, body=%wide.region_1.5_spmd.clone.sunk | while | flops 414790656 | bytes 51906808 | solution.py:97
  89.1 0.7 add_compare_fusion.2
  89.7 3.3 %constant_dynamic-slice_fusion.3 = (bf16[512,3072]{0,1:T(8,128)(2,1)S(1)}, bf16[512,3072]{0,1:T(8,128)(2,1)S(1)}) fusion(bf16[1536,3072]{0,1:T(8,128)(2,1)} %get-tuple-element.316, s32[]{:T(128)S(6)} %select_n.85, bf16[1536,3072]{0,1:T(8,128)(2,1)} %get-tuple-element.314), kind=kLoop, calls=%fused_computation.25.clone.1 | loop fusion | bytes 12582916 | tf_op jit(solution)/shard_map/while/body/eval_jaxpr/dynamic_slice | solution.py:86
  93.1 2.7 bitcast_reduce_fusion.2
  95.8 3.4 %fusion.74 = f32[32,64]{1,0:T(8,128)S(1)} fusion(f32[32,512,64]{1,2,0:T(8,128)} %get-tuple-element.282, f32[32,64]{1,0:T(8,128)S(1)} %get-tuple-element.310, pred[512]{0:T(512)(128)(4,1)S(1)} %add_compare_fusion.2), kind=kLoop, calls=%fused_computation.10.clone.1 | loop fusion | flops 4192256 | bytes 4211200 | tf_op jit(solution)/shard_map/while/body/eval_jaxpr/reduce_sum | solution.py:58
  99.3 2.5 fusion.76
  101.8 0.7 add_compare_fusion.2
  102.5 3.3 %constant_dynamic-slice_fusion.3 = (bf16[512,3072]{0,1:T(8,128)(2,1)S(1)}, bf16[512,3072]{0,1:T(8,128)(2,1)S(1)}) fusion(bf16[1536,3072]{0,1:T(8,128)(2,1)} %get-tuple-element.316, s32[]{:T(128)S(6)} %select_n.85, bf16[1536,3072]{0,1:T(8,128)(2,1)} %get-tuple-element.314), kind=kLoop, calls=%fused_computation.25.clone.1 | loop fusion | bytes 12582916 | tf_op jit(solution)/shard_map/while/body/eval_jaxpr/dynamic_slice | solution.py:86
  105.8 2.7 bitcast_reduce_fusion.2
  108.6 3.4 %fusion.74 = f32[32,64]{1,0:T(8,128)S(1)} fusion(f32[32,512,64]{1,2,0:T(8,128)} %get-tuple-element.282, f32[32,64]{1,0:T(8,128)S(1)} %get-tuple-element.310, pred[512]{0:T(512)(128)(4,1)S(1)} %add_compare_fusion.2), kind=kLoop, calls=%fused_computation.10.clone.1 | loop fusion | flops 4192256 | bytes 4211200 | tf_op jit(solution)/shard_map/while/body/eval_jaxpr/reduce_sum | solution.py:58
  112.0 3.5 %fusion.76 = f32[64,32,96]{2,0,1:T(8,128)} fusion(bf16[512,32,96]{0,2,1:T(8,128)(2,1)S(1)} %bitcast.119, f32[32,512,64]{1,2,0:T(8,128)S(1)} %copy-done, f32[32,64]{1,0:T(8,128)S(1)} %get-tuple-element.310, pred[512]{0:T(512)(128)(4,1)S(1)} %add_compare_fusion.2, f32[64,32,96]{2,0,1:T(8,128)} %get-tuple-element.300, ...), kind=kOutput, calls=%fused_computation.17.clone.1 | convolution fusion | flops 206110720 | bytes 8929793 | tf_op jit(solution)/shard_map/while/body/eval_jaxpr/hqk,khd->qhd/dot_general | solution.py:59
  115.5 0.7 add_compare_fusion.2
  116.2 3.3 %constant_dynamic-slice_fusion.3 = (bf16[512,3072]{0,1:T(8,128)(2,1)S(1)}, bf16[512,3072]{0,1:T(8,128)(2,1)S(1)}) fusion(bf16[1536,3072]{0,1:T(8,128)(2,1)} %get-tuple-element.316, s32[]{:T(128)S(6)} %select_n.85, bf16[1536,3072]{0,1:T(8,128)(2,1)} %get-tuple-element.314), kind=kLoop, calls=%fused_computation.25.clone.1 | loop fusion | bytes 12582916 | tf_op jit(solution)/shard_map/while/body/eval_jaxpr/dynamic_slice | solution.py:86
  119.5 2.7 bitcast_reduce_fusion.2
  122.3 3.4 %fusion.74 = f32[32,64]{1,0:T(8,128)S(1)} fusion(f32[32,512,64]{1,2,0:T(8,128)} %get-tuple-element.282, f32[32,64]{1,0:T(8,128)S(1)} %get-tuple-element.310, pred[512]{0:T(512)(128)(4,1)S(1)} %add_compare_fusion.2), kind=kLoop, calls=%fused_computation.10.clone.1 | loop fusion | flops 4192256 | bytes 4211200 | tf_op jit(solution)/shard_map/while/body/eval_jaxpr/reduce_sum | solution.py:58
  125.7 3.5 %fusion.76 = f32[64,32,96]{2,0,1:T(8,128)} fusion(bf16[512,32,96]{0,2,1:T(8,128)(2,1)S(1)} %bitcast.119, f32[32,512,64]{1,2,0:T(8,128)S(1)} %copy-done, f32[32,64]{1,0:T(8,128)S(1)} %get-tuple-element.310, pred[512]{0:T(512)(128)(4,1)S(1)} %add_compare_fusion.2, f32[64,32,96]{2,0,1:T(8,128)} %get-tuple-element.300, ...), kind=kOutput, calls=%fused_computation.17.clone.1 | convolution fusion | flops 206110720 | bytes 8929793 | tf_op jit(solution)/shard_map/while/body/eval_jaxpr/hqk,khd->qhd/dot_general | solution.py:59
  129.3 1.4 fusion.27
  130.7 2.7 fusion.24
  133.8 1.5 convert_element_type.80
  135.6 0.9 copy.43
  137.0 0.6 dynamic-slice
  138.5 37.9 %all-reduce = bf16[3072]{0:T(1024)(128)(2,1)S(1)} all-reduce(bf16[3072]{0:T(1024)(128)(2,1)S(1)} %dynamic-update-slice), channel_id=1, replica_groups=mesh['row'=8,'col'=16] {'col'}, use_global_device_ids=true, to_apply=%add | all-reduce | flops 3072 | bytes 12288
  176.5 0.6 reshape.232.gain_ref
  177.1 1.2 sort.17
  178.7 0.5 all_to_all.32
  179.3 0.7 convert_element_type.83
  180.0 0.8 fusion.19
  180.8 0.8 fusion.20
  181.7 1.5 copy.54
  183.2 8.7 %copy.42 = bf16[8192,384]{1,0:T(8,128)(2,1)} copy(bf16[8192,384]{0,1:T(8,128)(2,1)} %all-gather.13.cloned.1.call-done) | data formatting | bytes 12582912 | tf_op jit(solution)/shard_map/all_gather | solution.py:450
  191.9 2.8 all-gather.7.cloned.1.call-done
  194.7 5.7 %fusion.26.st_hbm = bf16[192,1024]{1,0:T(8,128)(2,1)} fusion(f32[1024,192]{0,1:T(8,128)S(1)} %copy.41, bf16[1024,3072]{1,0:T(8,128)(2,1)} %all-gather.7.cloned.1.call-done, bf16[192,3072]{1,0:T(8,128)(2,1)S(1)} %bitcast.132), kind=kOutput, calls=%fused_computation.41 | convolution fusion | flops 1208352768 | bytes 8650752 | tf_op jit(solution)/shard_map/dot_general | solution.py:456
  200.4 23.0 %all-gather.9.cloned.1.call-done.dn_hbm = bf16[3072,512]{1,0:T(8,128)(2,1)} async-done(((bf16[384,512]{1,0:T(8,128)(2,1)}), bf16[3072,512]{1,0:T(8,128)(2,1)}) %all-gather.9.cloned.1.call-update) | async-done | bytes 3145744 | tf_op jit(solution)/shard_map/all_gather | solution.py:453
  223.4 86.1 %mlp.1 = bf16[192,1024]{1,0:T(8,128)(2,1)} custom-call(bf16[192,1024]{1,0:T(8,128)(2,1)} %fusion.26.st_hbm, bf16[8,1024,384]{2,1,0:T(8,128)(2,1)} %bitcast.122, bf16[3072,512]{1,0:T(8,128)(2,1)} %all-gather.9.cloned.1.call-done.dn_hbm, bf16[8,1,384]{2,1,0:T(2,128)(2,1)} %reshape.232.gain_ref), custom_call_target="tpu_custom_call" | custom-call | tf_op jit(solution)/shard_map/mlp/pallas_call | solution.py:374
  309.5 1.2 copy.45
  310.7 0.6 gather_fusion.4
  311.4 0.9 copy.48
  (96 shorter events, 4.9 us)
Async XLA Ops:
  7.2 6.7 %copy-start.15 = (s32[1,16]{1,0:T(1,128)S(1)}, s32[1,16]{1,0:T(1,128)}, u32[]{:S(2)}) copy-start(s32[1,16]{1,0:T(1,128)} %param.20) | copy-start | bytes 196
  7.2 5.0 %copy-start.8 = (bf16[1024,192]{0,1:T(8,128)(2,1)S(1)}, bf16[1024,192]{0,1:T(8,128)(2,1)}, u32[]{:S(2)}) copy-start(bf16[1024,192]{0,1:T(8,128)(2,1)} %param.23) | copy-start | bytes 1179652
  7.2 5.8 %copy-start.9 = (bf16[1024,192]{0,1:T(8,128)(2,1)S(1)}, bf16[1024,192]{0,1:T(8,128)(2,1)}, u32[]{:S(2)}) copy-start(bf16[1024,192]{0,1:T(8,128)(2,1)} %param.21) | copy-start | bytes 1179652
  7.2 174.5 %all-gather.11.cloned.1.call-start = ((), (), s32[]{:S(2)}) async-start(), calls=%async_computation.5 | async-start | bytes 1327104 | tf_op jit(solution)/shard_map/all_gather | solution.py:449
  12.4 10.9 %copy-start.11 = (bf16[384,512]{1,0:T(8,128)(2,1)S(1)}, bf16[384,512]{1,0:T(8,128)(2,1)}, u32[]{:S(2)}) copy-start(bf16[384,512]{1,0:T(8,128)(2,1)} %param.34) | copy-start | bytes 1179652
  13.2 12.2 %copy-start.13 = (s32[1,64]{1,0:T(1,128)S(1)}, s32[1,64]{1,0:T(1,128)}, u32[]{:S(2)}) copy-start(s32[1,64]{1,0:T(1,128)} %param.28) | copy-start | bytes 772
  15.3 19.5 %all-to-all-start.1 = ((bf16[16,64,192]{2,1,0:T(8,128)(2,1)}), bf16[16,64,192]{2,1,0:T(8,128)(2,1)S(1)}, u32[]{:S(2)}, u32[]{:S(2)}) async-start(bf16[16,64,192]{2,1,0:T(8,128)(2,1)} %get-tuple-element.216), calls=%async_computation.1 | async-start | bytes 1048576 | tf_op jit(solution)/shard_map/all_to_all | solution.py:435
  23.3 159.9 %all-gather.13.cloned.1.call-start = ((), (), s32[]{:S(2)}) async-start(), calls=%async_computation.6 | async-start | bytes 7077888 | tf_op jit(solution)/shard_map/all_gather | solution.py:450
  34.8 29.3 %all-to-all-start = ((bf16[16,64,192]{2,1,0:T(8,128)(2,1)}), bf16[16,64,192]{2,1,0:T(8,128)(2,1)S(1)}, u32[]{:S(2)}, u32[]{:S(2)}) async-start(bf16[16,64,192]{2,1,0:T(8,128)(2,1)} %get-tuple-element.215), calls=%async_computation | async-start | bytes 1048576 | tf_op jit(solution)/shard_map/all_to_all | solution.py:434
  64.1 17.3 %all-to-all-start.2 = ((bf16[16,64,192]{2,1,0:T(8,128)(2,1)}), bf16[16,64,192]{2,1,0:T(8,128)(2,1)}, u32[]{:S(2)}, u32[]{:S(2)}) async-start(bf16[16,64,192]{2,1,0:T(8,128)(2,1)} %get-tuple-element.214), calls=%async_computation.2 | async-start | bytes 1048576 | tf_op jit(solution)/shard_map/all_to_all | solution.py:436
  71.3 123.4 %all-gather.7.cloned.1.call-start = ((), (), s32[]{:S(2)}) async-start(), calls=%async_computation.3 | async-start | bytes 6684672 | tf_op jit(solution)/shard_map/all_gather | solution.py:455
  82.8 1.8 copy-start.3
  87.7 1.4 copy-start.1
  87.7 1.4 copy-start.5
  89.7 3.3 %copy-start.2 = (bf16[64,32,96]{2,0,1:T(8,128)(2,1)S(1)}, bf16[64,32,96]{2,0,1:T(8,128)(2,1)}, u32[]{:S(2)}) copy-start(bf16[64,32,96]{2,0,1:T(8,128)(2,1)} %get-tuple-element.315) | copy-start | bytes 1179652 | tf_op jit(solution)/shard_map/while
  95.8 3.4 %copy-start = (f32[32,512,64]{1,2,0:T(8,128)S(1)}, f32[32,512,64]{1,2,0:T(8,128)}, u32[]{:S(2)}) copy-start(f32[32,512,64]{1,2,0:T(8,128)} %get-tuple-element.282) | copy-start | bytes 12582916 | tf_op jit(solution)/shard_map/while
  102.5 3.3 %copy-start.2 = (bf16[64,32,96]{2,0,1:T(8,128)(2,1)S(1)}, bf16[64,32,96]{2,0,1:T(8,128)(2,1)}, u32[]{:S(2)}) copy-start(bf16[64,32,96]{2,0,1:T(8,128)(2,1)} %get-tuple-element.315) | copy-start | bytes 1179652 | tf_op jit(solution)/shard_map/while
  108.5 3.4 %copy-start = (f32[32,512,64]{1,2,0:T(8,128)S(1)}, f32[32,512,64]{1,2,0:T(8,128)}, u32[]{:S(2)}) copy-start(f32[32,512,64]{1,2,0:T(8,128)} %get-tuple-element.282) | copy-start | bytes 12582916 | tf_op jit(solution)/shard_map/while
  116.2 3.3 %copy-start.2 = (bf16[64,32,96]{2,0,1:T(8,128)(2,1)S(1)}, bf16[64,32,96]{2,0,1:T(8,128)(2,1)}, u32[]{:S(2)}) copy-start(bf16[64,32,96]{2,0,1:T(8,128)(2,1)} %get-tuple-element.315) | copy-start | bytes 1179652 | tf_op jit(solution)/shard_map/while
  122.3 3.4 %copy-start = (f32[32,512,64]{1,2,0:T(8,128)S(1)}, f32[32,512,64]{1,2,0:T(8,128)}, u32[]{:S(2)}) copy-start(f32[32,512,64]{1,2,0:T(8,128)} %get-tuple-element.282) | copy-start | bytes 12582916 | tf_op jit(solution)/shard_map/while
  130.7 4.9 %copy-start.10 = (bf16[512,384]{1,0:T(8,128)(2,1)S(1)}, bf16[512,384]{1,0:T(8,128)(2,1)}, u32[]{:S(2)}) copy-start(bf16[512,384]{1,0:T(8,128)(2,1)} %param.35) | copy-start | bytes 1179652
  130.7 5.8 %copy-start.7 = (bf16[16,64,192]{2,1,0:T(8,128)(2,1)S(1)}, bf16[16,64,192]{2,1,0:T(8,128)(2,1)}, u32[]{:S(2)}) copy-start(bf16[16,64,192]{2,1,0:T(8,128)(2,1)} %get-tuple-element.217) | copy-start | bytes 1179652
  133.4 3.6 %copy-start.16 = (u32[128]{0:T(128)S(1)}, u32[128]{0:T(128)}, u32[]{:S(2)}) copy-start(u32[128]{0:T(128)} %constant.87) | copy-start | bytes 1540
  133.4 4.8 %copy-start.14 = (bf16[192]{0:T(256)(128)(2,1)S(1)}, bf16[192]{0:T(256)(128)(2,1)}, u32[]{:S(2)}) copy-start(bf16[192]{0:T(256)(128)(2,1)} %param.32) | copy-start | bytes 1156
  133.4 44.9 %copy-start.6 = (bf16[64,32,96]{2,0,1:T(8,128)(2,1)S(1)}, bf16[64,32,96]{2,0,1:T(8,128)(2,1)}, u32[]{:S(2)}) copy-start(bf16[64,32,96]{2,0,1:T(8,128)(2,1)} %copy-done.5) | copy-start | bytes 1179652
  133.4 45.3 %copy-start.4 = (bf16[64,16,192]{2,1,0:T(8,128)(2,1)S(1)}, bf16[64,16,192]{2,1,0:T(8,128)(2,1)}, u32[]{:S(2)}) copy-start(bf16[64,16,192]{2,1,0:T(8,128)(2,1)} %copy-done.3) | copy-start | bytes 1179652
  135.3 44.7 %copy-start.12 = (s32[1,8]{1,0:T(1,128)S(1)}, s32[1,8]{1,0:T(1,128)}, u32[]{:S(2)}) copy-start(s32[1,8]{1,0:T(1,128)} %param.30) | copy-start | bytes 100
  135.3 88.1 %all-gather.9.cloned.1.call-start = ((), (), s32[]{:S(2)}) async-start(), calls=%async_computation.4 | async-start | bytes 3538944 | tf_op jit(solution)/shard_map/all_gather | solution.py:453
Sparse Core Ops, SparseCore 0:
  9.7 25.9 all-gather.10
  37.4 40.9 all-gather.12
  135.4 59.1 all-gather.6
  196.2 27.1 all-gather.8

commit v2 on v1

--- a/solution.py
+++ b/solution.py
@@ -2,113 +2,393 @@
 
 import jax
 import jax.numpy as jnp
+import numpy as np
 from jax import lax
 from jax.experimental import pallas as pl
 from jax.experimental.pallas import tpu as pltpu
 from jax.sharding import PartitionSpec as P
 
 D = 3072
-HEADS = 32
 HEAD_DIM = 96
 MESH = pl.DeviceIdType.MESH
 
-
-def ancestry(parent_row):
-    count_all = parent_row.shape[0]
-    token_index = jnp.arange(count_all, dtype=jnp.int32)
-    linked = jnp.logical_or(
-        parent_row[:, None] == token_index[None, :], token_index[:, None] == token_index[None, :]
-    )
-    ancestors = linked.astype(jnp.float32)
-    for sweep in range(max(1, (count_all - 1).bit_length())):
-        ancestors = jnp.minimum(jnp.dot(ancestors, ancestors, precision=lax.Precision.HIGHEST), 1.0)
-    return ancestors
-
-
-def rotate(value_rows, position):
-    row_count = value_rows.shape[0]
-    half_dim = HEAD_DIM // 2
-    shaped = value_rows.astype(jnp.float32).reshape(row_count, HEADS, HEAD_DIM)
-    frequency = jnp.power(10000.0, -jnp.arange(half_dim, dtype=jnp.float32) * (2.0 / HEAD_DIM))
-    angles = position[:, None] * frequency[None, :]
-    cosine = jnp.cos(angles)[:, None, :]
-    sine_part = jnp.sin(angles)[:, None, :]
-    front_half = shaped[..., :half_dim]
-    back_half = shaped[..., half_dim:]
-    turned = jnp.concatenate(
-        [front_half * cosine - back_half * sine_part, back_half * cosine + front_half * sine_part],
-        axis=-1,
-    )
-    return turned.reshape(row_count, HEADS * HEAD_DIM).astype(jnp.bfloat16)
-
-
-def fold_block(state_now, q_heads, key_block, value_block, allowed):
-    running_max, row_totals, accumulator = state_now
-    score_scale = 1.0 / math.sqrt(HEAD_DIM)
-    key_heads = key_block.reshape(key_block.shape[0], HEADS, HEAD_DIM)
-    value_heads = value_block.reshape(value_block.shape[0], HEADS, HEAD_DIM)
-    scores = (
-        jnp.einsum("qhd,khd->hqk", q_heads, key_heads, preferred_element_type=jnp.float32)
-        * score_scale
-    )
-    scores = jnp.where(allowed[None], scores, -jnp.inf)
-    new_max = jnp.maximum(running_max, jnp.max(scores, axis=2))
-    rescale = jnp.exp(running_max - new_max)
-    weights = jnp.exp(scores - new_max[:, :, None])
-    row_totals = row_totals * rescale + jnp.sum(weights, axis=2)
-    mixed_rows = jnp.einsum(
-        "hqk,khd->qhd",
-        weights.astype(jnp.bfloat16),
-        value_heads,
-        preferred_element_type=jnp.float32,
-    )
-    accumulator = accumulator * rescale.T[:, :, None] + mixed_rows
-    return (new_max, row_totals, accumulator)
-
-
-def verify_slot(
-    query_rows, key_rows, value_rows, cache_k, cache_v, length, parent_row, live_count, path_row
+OFFS = (0, -1, 1, 2)
+HOPS = [
+    ((0, 0), 1, 1, None, (-1, 0)),
+    ((0, 0), 1, -1, None, (1, 0)),
+    ((-1, 0), 1, 1, 0, (2, 0)),
+    ((1, 0), 1, -1, 1, (2, 0)),
+]
+for _d in OFFS:
+    HOPS += [
+        ((_d, 0), 2, 1, None, (_d, -1)),
+        ((_d, 0), 2, -1, None, (_d, 1)),
+        ((_d, -1), 2, 1, 0, (_d, 2)),
+        ((_d, 1), 2, -1, 1, (_d, 2)),
+    ]
+
+
+def attend_kernel(
+    dealt_ref, length_ref, count_ref, parent_ref, path_ref, freq_ref, gain_ref,
+    q_ref, k_ref, v_ref, res_ref, wo_ref, gate_ref, up_ref, down_ref, ck_hbm, cv_hbm,
+    stream_ref, nk_ref, nv_ref, gains_ref, gu_out, dn_out,
+    KC, VC, SB, RB, ATT, PA, WO, TG, TD, turn, cosine, sine, anc_ref, RT,
+    kv_sem, loc_sem, x_send, x_recv, n_send, n_recv, w_send, w_recv, a_send, a_recv,
 ):
-    draft_rows = query_rows.shape[0]
-    width = query_rows.shape[1]
-    ancestors = ancestry(parent_row)
-    tree_depth = jnp.sum(ancestors, axis=1) - 1.0
-    position = length.astype(jnp.float32) + tree_depth
-    q_rot = rotate(query_rows, position)
-    k_rot = rotate(key_rows, position)
-    q_heads = q_rot.reshape(draft_rows, HEADS, HEAD_DIM)
-    cache_rows = cache_k.shape[0]
-    block_rows = min(512, cache_rows)
-
-    def cache_step(block_step, state_now):
-        block_start = block_step * block_rows
-        key_block = lax.dynamic_slice_in_dim(cache_k, block_start, block_rows, 0)
-        value_block = lax.dynamic_slice_in_dim(cache_v, block_start, block_rows, 0)
-        live_keys = block_start + jnp.arange(block_rows, dtype=jnp.int32) < length
-        allowed = jnp.broadcast_to(live_keys[None, :], (draft_rows, block_rows))
-        return fold_block(state_now, q_heads, key_block, value_block, allowed)
-
-    initial = (
-        jnp.full((HEADS, draft_rows), -jnp.inf, jnp.float32),
-        jnp.zeros((HEADS, draft_rows), jnp.float32),
-        jnp.zeros((draft_rows, HEADS, HEAD_DIM), jnp.float32),
-    )
-    block_total = cache_rows // block_rows
-    state_now = lax.fori_loop(0, block_total, cache_step, initial)
-    token_index = jnp.arange(draft_rows, dtype=jnp.int32)
-    allowed = jnp.logical_and(ancestors > 0.5, token_index[None, :] < live_count)
-    running_max, row_totals, accumulator = fold_block(
-        state_now, q_heads, k_rot, value_rows, allowed
-    )
-    attended = (
-        (accumulator / row_totals.T[:, :, None]).reshape(draft_rows, width).astype(jnp.bfloat16)
-    )
-    selector = (path_row[:, None] == token_index[None, :]).astype(jnp.bfloat16)
-    new_keys = jnp.dot(selector, k_rot, preferred_element_type=jnp.float32).astype(jnp.bfloat16)
-    new_values = jnp.dot(selector, value_rows, preferred_element_type=jnp.float32).astype(
-        jnp.bfloat16
-    )
-    return (attended, new_keys, new_values)
+    f32, bf = jnp.float32, jnp.bfloat16
+    row = lax.axis_index("row")
+    me = lax.axis_index("col")
+    z, x = me // 4, me % 4
+    y, core = row // 2, row % 2
+
+    def cache_in(p):
+        lanes = pl.ds(pl.multiple_of(p * 384, 128), 384)
+        return (
+            pltpu.make_async_copy(ck_hbm.at[0, :, lanes], KC.at[p], kv_sem.at[0, p]),
+            pltpu.make_async_copy(cv_hbm.at[0, :, lanes], VC.at[p], kv_sem.at[1, p]),
+        )
+
+    @pl.loop(0, 8)
+    def _(p):
+        for c in cache_in(p):
+            c.start()
+
+    barrier = pltpu.get_barrier_semaphore()
+
+    @pl.loop(1, 16)
+    def _(d):
+        pl.semaphore_signal(
+            barrier, inc=1, device_id={"col": (me + d) % 16}, device_id_type=MESH
+        )
+
+    row_up = ((y + 1) % 4) * 2 + core
+    row_down = ((y + 3) % 4) * 2 + core
+    row_twin = y * 2 + 1 - core
+    for r in (row_up, row_down, row_twin):
+        pl.semaphore_signal(barrier, inc=1, device_id={"row": r}, device_id_type=MESH)
+
+    @pl.loop(0, 16)
+    def _(j):
+        d = dealt_ref[0, j]
+        SB[j] = jnp.concatenate(
+            [q_ref[d], k_ref[d], v_ref[d], jnp.zeros((64, 64), bf)], axis=1
+        )
+
+    gains_ref[me] = gain_ref[...].astype(f32)
+    pl.semaphore_wait(barrier, 18)
+
+    def block_copy(j):
+        return pltpu.make_async_remote_copy(
+            src_ref=SB.at[j], dst_ref=RB.at[me], send_sem=x_send.at[j], recv_sem=x_recv.at[me],
+            device_id={"col": j}, device_id_type=MESH,
+        )
+
+    def block_arrival(s):
+        return pltpu.make_async_remote_copy(
+            src_ref=SB.at[s], dst_ref=RB.at[s], send_sem=x_send.at[s], recv_sem=x_recv.at[s],
+            device_id={"col": s}, device_id_type=MESH,
+        )
+
+    def gain_copy(j, slot):
+        return pltpu.make_async_remote_copy(
+            src_ref=gains_ref.at[me], dst_ref=gains_ref.at[slot],
+            send_sem=n_send.at[j], recv_sem=n_recv.at[slot],
+            device_id={"col": j}, device_id_type=MESH,
+        )
+
+    RB[me] = SB[me]
+
+    @pl.loop(1, 16)
+    def _(d):
+        j = (me + d) % 16
+        block_copy(j).start()
+        gain_copy(j, me).start()
+
+    WO[row] = wo_ref[...].astype(f32).T.astype(bf)
+    TG[0:512] = gate_ref[...].astype(f32).T.astype(bf)
+    TG[512:1024] = up_ref[...].astype(f32).T.astype(bf)
+    TD[...] = down_ref[...].astype(f32).T.astype(bf)
+    own_gu = pltpu.make_async_copy(TG, gu_out.at[row], loc_sem.at[0])
+    own_dn = pltpu.make_async_copy(TD, dn_out.at[row], loc_sem.at[1])
+    own_gu.start()
+    own_dn.start()
+    tables = ((WO, None, 192), (gu_out, TG, 1024), (dn_out, TD, 384))
+    yb = {
+        0: row, -1: row_down, 1: row_up, 2: ((y + 2) % 4) * 2 + core,
+    }
+    wmoves = [
+        (0, None, row_up, -1, False),
+        (0, None, row_down, 1, False),
+        (-1, 0, row_up, 2, False),
+        (1, 1, row_down, 2, False),
+        (0, None, row_twin, 0, True),
+        (-1, None, row_twin, -1, True),
+        (1, None, row_twin, 1, True),
+        (2, None, row_twin, 2, True),
+    ]
+
+    def wref(t, index, part, own):
+        table, mine, size = tables[t]
+        if own and mine is not None:
+            return mine
+        if part is None:
+            return table.at[index]
+        return table.at[index, pl.ds(part * (size // 2), size // 2)]
+
+    def wmove(t, k):
+        d, part, target, _, _ = wmoves[k]
+        return pltpu.make_async_remote_copy(
+            src_ref=wref(t, yb[d], part, d == 0), dst_ref=wref(t, yb[d], part, False),
+            send_sem=w_send.at[t, k], recv_sem=w_recv.at[t, k],
+            device_id={"row": target}, device_id_type=MESH,
+        )
+
+    def wgot(t, k):
+        _, part, target, d, twin = wmoves[k]
+        index = yb[d] + 1 - 2 * core if twin else yb[d]
+        ref = wref(t, index, part, False)
+        pltpu.make_async_remote_copy(
+            src_ref=ref, dst_ref=ref, send_sem=w_send.at[t, k], recv_sem=w_recv.at[t, k],
+            device_id={"row": target}, device_id_type=MESH,
+        ).wait_recv()
+
+    for t in range(3):
+        for k in (0, 1, 4):
+            wmove(t, k).start()
+
+    i64 = lax.broadcasted_iota(jnp.int32, (64, 64), 0)
+    j64 = lax.broadcasted_iota(jnp.int32, (64, 64), 1)
+    anc = jnp.logical_or(parent_ref[...] == j64, i64 == j64).astype(f32)
+    for sweep in range(6):
+        half = anc.astype(bf)
+        anc = jnp.minimum(jnp.dot(half, half, preferred_element_type=f32), 1.0)
+    length = length_ref[0]
+    live = count_ref[0]
+    position = length.astype(f32) + jnp.sum(anc, axis=1, keepdims=True) - 1.0
+    angle = position * freq_ref[...]
+    cosine[...] = jnp.cos(angle)
+    sine[...] = jnp.sin(angle)
+    anc_ref[...] = jnp.where(j64 < live, anc, 0.0)
+    ti = lax.broadcasted_iota(jnp.int32, (192, 192), 0)
+    tj = lax.broadcasted_iota(jnp.int32, (192, 192), 1)
+    low = (tj % 96) < 48
+    turn[...] = jnp.where(
+        jnp.logical_and(low, ti == tj + 48), -1.0,
+        jnp.where(jnp.logical_and(jnp.logical_not(low), ti == tj - 48), 1.0, 0.0),
+    ).astype(bf)
+
+    @pl.loop(0, 8)
+    def _(m):
+        pair = jnp.concatenate(
+            [res_ref[dealt_ref[0, 2 * m]], res_ref[dealt_ref[0, 2 * m + 1]]], axis=0
+        ).astype(f32)
+        RT[:, pl.ds(pl.multiple_of(m * 128, 128), 128)] = pair.T
+
+    def rotated(rows):
+        swapped = jnp.dot(rows, turn[...], preferred_element_type=f32)
+        return (rows.astype(f32) * cosine[...] + swapped * sine[...]).astype(bf)
+
+    a_own, b_own = (x, z), (z, x)
+
+    def at(h, da, db):
+        a, b = (a_own[h] + da + 4) % 4, (b_own[h] + db + 4) % 4
+        return b * 4 + a if h == 0 else a * 4 + b
+
+    def piece(p, c, part):
+        return ATT.at[p, c] if part is None else ATT.at[p, c, pl.ds(32 * part, 32)]
+
+    def amove(p, h, k):
+        (da, db), axis, way, part, _ = HOPS[k]
+        ref = piece(p, at(h, da, db), part)
+        target = at(h, way, 0) if axis == 1 else at(h, 0, way)
+        return pltpu.make_async_remote_copy(
+            src_ref=ref, dst_ref=ref, send_sem=a_send.at[p, k], recv_sem=a_recv.at[p, k],
+            device_id={"col": target}, device_id_type=MESH,
+        )
+
+    def agot(p, h, k):
+        _, axis, way, part, (da, db) = HOPS[k]
+        ref = piece(p, at(h, da, db), part)
+        target = at(h, way, 0) if axis == 1 else at(h, 0, way)
+        pltpu.make_async_remote_copy(
+            src_ref=ref, dst_ref=ref, send_sem=a_send.at[p, k], recv_sem=a_recv.at[p, k],
+            device_id={"col": target}, device_id_type=MESH,
+        ).wait_recv()
+
+    nt = (((1,), (1,)), ((), ()))
+    scale = 1.0 / math.sqrt(HEAD_DIM)
+    head_of_lane = lax.broadcasted_iota(jnp.int32, (64, 384), 1) // 96
+    key_live = lax.broadcasted_iota(jnp.int32, (1, 1536), 1) < length
+    path_hot = (
+        path_ref[...] == lax.broadcasted_iota(jnp.int32, (8, 64), 1)
+    ).astype(f32).astype(bf)
+
+    def chunk(p, h):
+        for e in range(2):
+            @pl.when(2 * p + e != me)
+            def _(e=e):
+                block_arrival(2 * p + e).wait_recv()
+        first, other = RB[2 * p], RB[2 * p + 1]
+        q = jnp.concatenate([rotated(first[:, 0:192]), rotated(other[:, 0:192])], axis=1)
+        kd = jnp.concatenate([rotated(first[:, 192:384]), rotated(other[:, 192:384])], axis=1)
+        vd = jnp.concatenate([first[:, 384:576], other[:, 384:576]], axis=1)
+        lanes = pl.ds(pl.multiple_of(p * 384, 128), 384)
+        nk_ref[0, :, lanes] = jnp.dot(path_hot, kd, preferred_element_type=f32).astype(bf)
+        nv_ref[0, :, lanes] = jnp.dot(path_hot, vd, preferred_element_type=f32).astype(bf)
+        wide = jnp.concatenate(
+            [jnp.where(head_of_lane == n, q, jnp.zeros_like(q)) for n in range(4)], axis=0
+        )
+        for c in cache_in(p):
+            c.wait()
+        old = lax.dot_general(wide, KC[p], nt, preferred_element_type=f32)
+        old = jnp.where(key_live, old, -jnp.inf)
+        new = lax.dot_general(wide, kd, nt, preferred_element_type=f32)
+        allowed = jnp.concatenate([anc_ref[...]] * 4, axis=0) > 0.5
+        new = jnp.where(allowed, new, -jnp.inf)
+        top = jnp.maximum(
+            jnp.max(old, axis=1, keepdims=True), jnp.max(new, axis=1, keepdims=True)
+        )
+        w_old = jnp.exp((old - top) * scale)
+        w_new = jnp.exp((new - top) * scale)
+        total = jnp.sum(w_old, axis=1, keepdims=True) + jnp.sum(w_new, axis=1, keepdims=True)
+        mixed = jnp.dot(w_old.astype(bf), VC[p], preferred_element_type=f32) + jnp.dot(
+            w_new.astype(bf), vd, preferred_element_type=f32
+        )
+        mixed = mixed / total
+        attended = jnp.zeros((64, 384), f32)
+        for n in range(4):
+            attended = jnp.where(head_of_lane == n, mixed[64 * n : 64 * n + 64], attended)
+        ATT[p, me] = attended.astype(bf)
+        for k in (0, 1, 4, 5):
+            amove(p, h, k).start()
+
+    @pl.loop(0, 4)
+    def _(g):
+        for h in range(2):
+            chunk(2 * g + h, h)
+
+    def forward(t):
+        wgot(t, 0)
+        wmove(t, 2).start()
+        wmove(t, 5).start()
+        wgot(t, 1)
+        wmove(t, 3).start()
+        wmove(t, 6).start()
+
+    def last(t):
+        wgot(t, 2)
+        wgot(t, 3)
+        wmove(t, 7).start()
+
+    def stage(moves):
+        @pl.loop(0, 4)
+        def _(g):
+            for h in range(2):
+                for waits, starts in moves:
+                    for k in waits:
+                        agot(2 * g + h, h, k)
+                    for k in starts:
+                        amove(2 * g + h, h, k).start()
+
+    forward(0)
+    stage([((0,), (2, 8, 9)), ((1,), (3, 12, 13))])
+    forward(1)
+    stage([((4,), (6,)), ((5,), (7,)), ((2, 3), (16, 17))])
+    last(0)
+    forward(2)
+    stage([((8,), (10,)), ((9,), (11,)), ((12,), (14,)), ((13,), (15,))])
+    stage([((16,), (18,)), ((17,), (19,))])
+    last(1)
+    PA[...] = RT[...]
+    for k in (4, 5, 6, 7):
+        wgot(0, k)
+
+    @pl.loop(0, 4)
+    def _(g):
+        for h in range(2):
+            p = 2 * g + h
+            for k in (6, 7, 10, 11, 14, 15, 18, 19):
+                agot(p, h, k)
+            PA[...] += lax.dot_general(
+                WO[p], ATT[p].reshape(1024, 384), nt, preferred_element_type=f32
+            )
+
+    stream_ref[...] = PA[...].astype(bf)
+    last(2)
+    for t in (1, 2):
+        for k in (4, 5, 6, 7):
+            wgot(t, k)
+
+    @pl.loop(1, 16)
+    def _(d):
+        j = (me + d) % 16
+        block_copy(j).wait_send()
+        gain_copy(j, me).wait_send()
+        gain_copy(j, j).wait_recv()
+
+    for t in range(3):
+        for k in range(8):
+            wmove(t, k).wait_send()
+
+    @pl.loop(0, 4)
+    def _(g):
+        for h in range(2):
+            for k in range(20):
+                amove(2 * g + h, h, k).wait_send()
+
+    own_gu.wait()
+    own_dn.wait()
+
+
+def attend_call(dealing, lengths, counts, parent_col, path_col, freq, gain, q, k, v, res, wo, gate, up, down, ck, cv):
+    anyspace = pl.BlockSpec(memory_space=pl.ANY)
+    vmem = pl.BlockSpec(memory_space=pltpu.VMEM)
+    smem = pl.BlockSpec(memory_space=pltpu.SMEM)
+    bf, f32 = jnp.bfloat16, jnp.float32
+    dma = pltpu.SemaphoreType.DMA
+    return pl.pallas_call(
+        attend_kernel,
+        out_shape=(
+            jax.ShapeDtypeStruct((192, 1024), bf),
+            jax.ShapeDtypeStruct((1, 8, 3072), bf),
+            jax.ShapeDtypeStruct((1, 8, 3072), bf),
+            jax.ShapeDtypeStruct((16, 1, 192), f32),
+            jax.ShapeDtypeStruct((8, 1024, 384), bf),
+            jax.ShapeDtypeStruct((8, 384, 512), bf),
+        ),
+        in_specs=[smem] * 3 + [vmem] * 12 + [anyspace] * 2,
+        out_specs=(vmem, vmem, vmem, vmem, anyspace, anyspace),
+        scratch_shapes=[
+            pltpu.VMEM((8, 1536, 384), bf),
+            pltpu.VMEM((8, 1536, 384), bf),
+            pltpu.VMEM((16, 64, 640), bf),
+            pltpu.VMEM((16, 64, 640), bf),
+            pltpu.VMEM((8, 16, 64, 384), bf),
+            pltpu.VMEM((192, 1024), f32),
+            pltpu.VMEM((8, 192, 384), bf),
+            pltpu.VMEM((1024, 384), bf),
+            pltpu.VMEM((384, 512), bf),
+            pltpu.VMEM((192, 192), bf),
+            pltpu.VMEM((64, 192), f32),
+            pltpu.VMEM((64, 192), f32),
+            pltpu.VMEM((64, 64), f32),
+            pltpu.VMEM((192, 1024), f32),
+            dma((2, 8)),
+            dma((2,)),
+            dma((16,)),
+            dma((16,)),
+            dma((16,)),
+            dma((16,)),
+            dma((3, 8)),
+            dma((3, 8)),
+            dma((8, 20)),
+            dma((8, 20)),
+        ],
+        compiler_params=pltpu.CompilerParams(
+            collective_id=1, has_side_effects=True, vmem_limit_bytes=60 * 1024 * 1024
+        ),
+        name="attend",
+    )(dealing, lengths, counts, parent_col, path_col, freq, gain, q, k, v, res, wo, gate, up, down, ck, cv)
 
 
 def mlp_kernel(
@@ -183,7 +463,8 @@
 
     @pl.loop(0, 8)
     def _(r):
-        W[r] = W[r] * gain_ref[r]
+        both = jnp.concatenate([gain_ref[2 * r], gain_ref[2 * r + 1]], axis=1)
+        W[r] = W[r] * both.astype(jnp.bfloat16)
 
     for h in halves:
         arrived(h, 0, at(h, -1, 0))
@@ -421,51 +702,34 @@
     up_weight,
     down_weight,
 ):
-    columns = lax.axis_size("col")
-    dealt_order = dealing[0]
-    rows_here = residual.shape[0]
-    draft_rows = rows_here // columns
-
-    def to_slots(block_rows):
-        shaped = block_rows.reshape(columns, draft_rows, block_rows.shape[1])
-        return jnp.take(shaped, dealt_order, axis=0).reshape(rows_here, block_rows.shape[1])
-
-    mine_q, mine_k, mine_v = (
-        lax.all_to_all(to_slots(queries), "col", split_axis=0, concat_axis=1, tiled=True),
-        lax.all_to_all(to_slots(draft_keys), "col", split_axis=0, concat_axis=1, tiled=True),
-        lax.all_to_all(to_slots(draft_values), "col", split_axis=0, concat_axis=1, tiled=True),
+    freq = np.power(10000.0, -(np.arange(192) % 48) * (2.0 / HEAD_DIM)).astype(np.float32)
+
+    def by_request(rows):
+        return rows.reshape(16, 64, 192)
+
+    stream_t, new_keys, new_values, gains, gate_up, down_t = attend_call(
+        dealing,
+        cache_lengths,
+        draft_counts,
+        parents.reshape(64, 1),
+        accepted.reshape(8, 1),
+        jnp.asarray(freq).reshape(1, 192),
+        norm_gain.reshape(1, 192),
+        by_request(queries),
+        by_request(draft_keys),
+        by_request(draft_values),
+        by_request(residual),
+        out_weight,
+        gate_weight,
+        up_weight,
+        down_weight,
+        cache_keys,
+        cache_values,
     )
-    attended, new_keys, new_values = verify_slot(
-        mine_q,
-        mine_k,
-        mine_v,
-        cache_keys[0],
-        cache_values[0],
-        cache_lengths[0],
-        parents[0],
-        draft_counts[0],
-        accepted[0],
-    )
-    wo_t = lax.all_gather(out_weight.T[None], "row", axis=0, tiled=True)
-    gate_up = lax.all_gather(
-        jnp.concatenate([gate_weight.T, up_weight.T], axis=0)[None], "row", axis=0, tiled=True
-    )
-    down_t = lax.all_gather(down_weight.T, "row", axis=0, tiled=True)
-    gain = lax.all_gather(norm_gain, "col", axis=0, tiled=True).reshape(8, 1, 384)
-    every = lax.all_gather(attended, "col", axis=0, tiled=True)
-    projected = lax.dot_general(
-        jnp.transpose(wo_t, (1, 0, 2)).reshape(192, 3072),
-        every,
-        (((1,), (1,)), ((), ())),
-        preferred_element_type=jnp.float32,
-    )
-    stream_t = (to_slots(residual).T.astype(jnp.float32) + projected).astype(jnp.bfloat16)
-    out_t = mlp_call(stream_t, gate_up, down_t, gain)
-    inverse = jnp.argsort(dealt_order)
-    layer_out = jnp.take(out_t.T.reshape(columns, draft_rows, 192), inverse, axis=0).reshape(
-        rows_here, 192
-    )
-    return (layer_out, new_keys[None], new_values[None])
+    out_t = mlp_call(stream_t, gate_up, down_t.reshape(3072, 512), gains)
+    inverse = jnp.argsort(dealing[0])
+    layer_out = jnp.take(out_t.T.reshape(16, 64, 192), inverse, axis=0).reshape(1024, 192)
+    return (layer_out, new_keys, new_values)
 
 
 def solution(mesh):

time: 321 us -> 187 us (0.58)
  Pallas kernels: 86.1 us -> 165 us
  local copies, waits for them, and re-layouts: 64.4 us -> 17.8 us
  waiting for transfers between devices: 41.4 us -> 0 us
  blocking collectives: 37.9 us -> 0 us
  matrix products: 30.4 us -> 0 us
  other arithmetic: 22.8 us -> 1.47 us
  starting transfers between devices: 19.3 us -> 0 us
  between operations: 16.3 us -> 2.02 us
    pallas_call x0 -> x1, Pallas kernels: none -> 76.5 us  [attend_call(): pl.pallas_call(attend_kernel, out_shape=(jax.ShapeDtypeStruct((192, 1024)...]
    unnamed x1 -> x0, blocking collectives: 37.9 us -> none
    dot_general x17 -> x0, matrix products: 30.4 us -> none  [the longest x4 12.2 us: fold_block(): jnp.einsum('hqk,khd->qhd', weights.astype(jnp.bfloat16), value_heads, pre...]
    all_gather x4 -> x0, waiting for transfers between devices: 25.8 us -> none  [the longest x1 23 us: body(): down_t = lax.all_gather(down_weight.T, 'row', axis=0, tiled=True)]
    unnamed x42 -> x14, local copies, waits for them, and re-layouts: 32.5 us -> 11.9 us
    all_to_all x3 -> x0, starting transfers between devices: 18.7 us -> none  [the longest x1 7.99 us: body(): lax.all_to_all(to_slots(draft_keys), 'col', split_axis=0, concat_axis=1,...]
    all_to_all x3 -> x0, waiting for transfers between devices: 14.9 us -> none  [the longest x1 8 us: body(): lax.all_to_all(to_slots(draft_values), 'col', split_axis=0, concat_axis=1...]
    reduce_sum x4 -> x0, other arithmetic: 11.6 us -> none  [fold_block(): row_totals = row_totals * rescale + jnp.sum(weights, axis=2)]
  transfers between devices with their start and end apart: 7 -> 0, of which waited for: 4 -> 0; matrix products, arithmetic and copies ran while one was open for 36% -> 0% of each run, Pallas kernels for 0% -> 0%
where the time goes in v2:
time: 187 us; the launch traced here: 186 us
  Pallas kernels  165 us (88%)
  local copies, waits for them, and re-layouts  17.8 us (10%)
  between operations  2.02 us (1%)
    pallas_call x1, Pallas kernels, mlp_call(): pl.pallas_call(mlp_kernel, out_shape=jax.ShapeDtypeStruct((192, 1024), bf...  88.7 us
    pallas_call x1, Pallas kernels, attend_call(): pl.pallas_call(attend_kernel, out_shape=(jax.ShapeDtypeStruct((192, 1024)...  76.5 us
    unnamed x14, local copies, waits for them, and re-layouts  11.9 us

profile of v2, /device:TPU:0, one launch (start us, length us, event | category | flops | bytes accessed | tf_op | source)
XLA Modules:
  0.0 186.4 jit_solution(9362403294179670756)
XLA Ops:
  0.6 2.0 %copy.27 = bf16[1024,192]{1,0:T(8,128)(2,1)} copy(bf16[1024,192]{0,1:T(8,128)(2,1)} %param.19) | data formatting | bytes 786432 | tf_op args[2]
  2.6 2.0 %copy.28 = bf16[1024,192]{1,0:T(8,128)(2,1)} copy(bf16[1024,192]{0,1:T(8,128)(2,1)} %param.20) | data formatting | bytes 786432 | tf_op args[3]
  4.6 2.0 %copy.29 = bf16[1024,192]{1,0:T(8,128)(2,1)} copy(bf16[1024,192]{0,1:T(8,128)(2,1)} %param.21) | data formatting | bytes 786432 | tf_op args[4]
  6.6 2.0 %copy.30 = bf16[1024,192]{1,0:T(8,128)(2,1)} copy(bf16[1024,192]{0,1:T(8,128)(2,1)} %param.18) | data formatting | bytes 786432 | tf_op args[1]
  8.7 1.7 copy.33.wo_ref
  10.4 1.4 copy.31.parent_ref
  11.7 1.3 copy.32.path_ref
  13.1 1.2 reshape.47.gain_ref
  15.6 76.5 %attend.1 = (bf16[192,1024]{1,0:T(8,128)(2,1)}, bf16[1,8,3072]{2,1,0:T(8,128)(2,1)}, bf16[1,8,3072]{2,1,0:T(8,128)(2,1)}, f32[16,1,192]{2,1,0:T(1,128)}, bf16[8,...) custom-call(s32[1,16]{1,0:T(1,128)} %dealt_ref.1, s32[1]{0:T(128)S(6)} %copy.38.length_ref, s32[1]{0:T(128)S(6)} %copy.39.count_ref, ...), custom_call_target="tpu_custom_call" | custom-call | tf_op jit(solution)/shard_map/attend/pallas_call | solution.py:349
  92.1 0.0 copy-start.2
  92.1 0.0 copy-start.1
  92.1 0.0 copy-start
  92.1 88.7 %mlp.1 = bf16[192,1024]{1,0:T(8,128)(2,1)} custom-call(bf16[192,1024]{1,0:T(8,128)(2,1)} %get-tuple-element.11.st_hbm, bf16[8,1024,384]{2,1,0:T(8,128)(2,1)} %get-tuple-element.12.w_hbm, bf16[3072,512]{1,0:T(8,128)(2,1)} %bitcast.12, f32[16,1,192]{2,1,0:T(1,128)} %get-tuple-element.14.gain_ref), custom_call_target="tpu_custom_call" | custom-call | tf_op jit(solution)/shard_map/mlp/pallas_call | solution.py:655
  180.8 1.2 copy.34
  182.0 0.0 copy-done.2
  182.0 1.2 sort.17
  183.3 0.6 gather_fusion
  183.9 0.1 broadcast_in_dim.16
  184.0 0.1 broadcast_in_dim.17
  184.0 0.2 bitcast_select_fusion
  184.3 0.9 copy.35
  185.2 0.0 copy-done.1
  185.2 0.6 copy.40
  185.8 0.0 copy-done
  185.8 0.6 copy.41
  (4 shorter events, 0.0 us)
Async XLA Ops:
  92.1 89.9 %copy-start.2 = (s32[1,16]{1,0:T(1,128)S(1)}, s32[1,16]{1,0:T(1,128)}, u32[]{:S(2)}) copy-start(s32[1,16]{1,0:T(1,128)} %dealt_ref.1) | copy-start | bytes 196
  92.1 93.1 %copy-start.1 = (bf16[1,8,3072]{2,1,0:T(8,128)(2,1)S(1)}, bf16[1,8,3072]{2,1,0:T(8,128)(2,1)}, u32[]{:S(2)}) copy-start(bf16[1,8,3072]{2,1,0:T(8,128)(2,1)} %get-tuple-element.24) | copy-start | bytes 147460
  92.1 93.7 %copy-start = (bf16[1,8,3072]{2,1,0:T(8,128)(2,1)S(1)}, bf16[1,8,3072]{2,1,0:T(8,128)(2,1)}, u32[]{:S(2)}) copy-start(bf16[1,8,3072]{2,1,0:T(8,128)(2,1)} %get-tuple-element.25) | copy-start | bytes 147460

commit v3 on v2

--- a/solution.py
+++ b/solution.py
@@ -32,7 +32,7 @@
     dealt_ref, length_ref, count_ref, parent_ref, path_ref, freq_ref, gain_ref,
     q_ref, k_ref, v_ref, res_ref, wo_ref, gate_ref, up_ref, down_ref, ck_hbm, cv_hbm,
     stream_ref, nk_ref, nv_ref, gains_ref, gu_out, dn_out,
-    KC, VC, SB, RB, ATT, PA, WO, TG, TD, turn, cosine, sine, anc_ref, RT,
+    KC, VC, SB, RB, ATT, PA, WO, TG, TD, turn, cosine, sine, anc_ref, TT, RB1,
     kv_sem, loc_sem, x_send, x_recv, n_send, n_recv, w_send, w_recv, a_send, a_recv,
 ):
     f32, bf = jnp.float32, jnp.bfloat16
@@ -67,14 +67,19 @@
     for r in (row_up, row_down, row_twin):
         pl.semaphore_signal(barrier, inc=1, device_id={"row": r}, device_id_type=MESH)
 
+    for n, ref in enumerate((q_ref, k_ref, v_ref)):
+        for m in range(4):
+            rows = ref[:, 256 * m : 256 * m + 256].astype(f32).T.astype(bf)
+            TT[4 * m : 4 * m + 4, :, 192 * n : 192 * n + 192] = rows.reshape(4, 64, 192)
+
     @pl.loop(0, 16)
     def _(j):
-        d = dealt_ref[0, j]
-        SB[j] = jnp.concatenate(
-            [q_ref[d], k_ref[d], v_ref[d], jnp.zeros((64, 64), bf)], axis=1
-        )
-
-    gains_ref[me] = gain_ref[...].astype(f32)
+        block = TT[dealt_ref[0, j]]
+        for n in range(4):
+            SB[j, 64 * n : 64 * n + 64] = block[:, 128 * n : 128 * n + 128]
+        SB[j, 256:288] = jnp.concatenate([block[0:32, 512:576], block[32:64, 512:576]], axis=1)
+
+    gains_ref[me] = gain_ref[...].astype(f32).reshape(1, 192)
     pl.semaphore_wait(barrier, 18)
 
     def block_copy(j):
@@ -104,7 +109,7 @@
         block_copy(j).start()
         gain_copy(j, me).start()
 
-    WO[row] = wo_ref[...].astype(f32).T.astype(bf)
+    WO[row] = wo_ref[...]
     TG[0:512] = gate_ref[...].astype(f32).T.astype(bf)
     TG[512:1024] = up_ref[...].astype(f32).T.astype(bf)
     TD[...] = down_ref[...].astype(f32).T.astype(bf)
@@ -158,10 +163,11 @@
 
     i64 = lax.broadcasted_iota(jnp.int32, (64, 64), 0)
     j64 = lax.broadcasted_iota(jnp.int32, (64, 64), 1)
-    anc = jnp.logical_or(parent_ref[...] == j64, i64 == j64).astype(f32)
+    anc = jnp.logical_or(parent_ref[...] == i64, i64 == j64).astype(f32)
     for sweep in range(6):
         half = anc.astype(bf)
         anc = jnp.minimum(jnp.dot(half, half, preferred_element_type=f32), 1.0)
+    anc = anc.T
     length = length_ref[0]
     live = count_ref[0]
     position = length.astype(f32) + jnp.sum(anc, axis=1, keepdims=True) - 1.0
@@ -177,12 +183,13 @@
         jnp.where(jnp.logical_and(jnp.logical_not(low), ti == tj - 48), 1.0, 0.0),
     ).astype(bf)
 
+    for j in range(16):
+        RB1[j] = res_ref[:, 64 * j : 64 * j + 64]
+
     @pl.loop(0, 8)
     def _(m):
-        pair = jnp.concatenate(
-            [res_ref[dealt_ref[0, 2 * m]], res_ref[dealt_ref[0, 2 * m + 1]]], axis=0
-        ).astype(f32)
-        RT[:, pl.ds(pl.multiple_of(m * 128, 128), 128)] = pair.T
+        pair = jnp.concatenate([RB1[dealt_ref[0, 2 * m]], RB1[dealt_ref[0, 2 * m + 1]]], axis=1)
+        PA[:, pl.ds(pl.multiple_of(m * 128, 128), 128)] = pair.astype(f32)
 
     def rotated(rows):
         swapped = jnp.dot(rows, turn[...], preferred_element_type=f32)
@@ -220,15 +227,20 @@
     head_of_lane = lax.broadcasted_iota(jnp.int32, (64, 384), 1) // 96
     key_live = lax.broadcasted_iota(jnp.int32, (1, 1536), 1) < length
     path_hot = (
-        path_ref[...] == lax.broadcasted_iota(jnp.int32, (8, 64), 1)
-    ).astype(f32).astype(bf)
+        (path_ref[...] == lax.broadcasted_iota(jnp.int32, (64, 8), 0)).astype(f32).T.astype(bf)
+    )
 
     def chunk(p, h):
         for e in range(2):
             @pl.when(2 * p + e != me)
             def _(e=e):
                 block_arrival(2 * p + e).wait_recv()
-        first, other = RB[2 * p], RB[2 * p + 1]
+        def unpack(s):
+            block = RB[s]
+            tail = jnp.concatenate([block[256:288, 0:64], block[256:288, 64:128]], axis=0)
+            return jnp.concatenate([block[64 * n : 64 * n + 64] for n in range(4)] + [tail], axis=1)
+
+        first, other = unpack(2 * p), unpack(2 * p + 1)
         q = jnp.concatenate([rotated(first[:, 0:192]), rotated(other[:, 0:192])], axis=1)
         kd = jnp.concatenate([rotated(first[:, 192:384]), rotated(other[:, 192:384])], axis=1)
         vd = jnp.concatenate([first[:, 384:576], other[:, 384:576]], axis=1)
@@ -299,7 +311,6 @@
     stage([((8,), (10,)), ((9,), (11,)), ((12,), (14,)), ((13,), (15,))])
     stage([((16,), (18,)), ((17,), (19,))])
     last(1)
-    PA[...] = RT[...]
     for k in (4, 5, 6, 7):
         wgot(0, k)
 
@@ -340,7 +351,7 @@
     own_dn.wait()
 
 
-def attend_call(dealing, lengths, counts, parent_col, path_col, freq, gain, q, k, v, res, wo, gate, up, down, ck, cv):
+def attend_call(dealing, lengths, counts, parents, path, freq, gain, q, k, v, res, wo, gate, up, down, ck, cv):
     anyspace = pl.BlockSpec(memory_space=pl.ANY)
     vmem = pl.BlockSpec(memory_space=pltpu.VMEM)
     smem = pl.BlockSpec(memory_space=pltpu.SMEM)
@@ -361,8 +372,8 @@
         scratch_shapes=[
             pltpu.VMEM((8, 1536, 384), bf),
             pltpu.VMEM((8, 1536, 384), bf),
-            pltpu.VMEM((16, 64, 640), bf),
-            pltpu.VMEM((16, 64, 640), bf),
+            pltpu.VMEM((16, 288, 128), bf),
+            pltpu.VMEM((16, 288, 128), bf),
             pltpu.VMEM((8, 16, 64, 384), bf),
             pltpu.VMEM((192, 1024), f32),
             pltpu.VMEM((8, 192, 384), bf),
@@ -372,7 +383,8 @@
             pltpu.VMEM((64, 192), f32),
             pltpu.VMEM((64, 192), f32),
             pltpu.VMEM((64, 64), f32),
-            pltpu.VMEM((192, 1024), f32),
+            pltpu.VMEM((16, 64, 640), bf),
+            pltpu.VMEM((16, 192, 64), bf),
             dma((2, 8)),
             dma((2,)),
             dma((16,)),
@@ -388,12 +400,12 @@
             collective_id=1, has_side_effects=True, vmem_limit_bytes=60 * 1024 * 1024
         ),
         name="attend",
-    )(dealing, lengths, counts, parent_col, path_col, freq, gain, q, k, v, res, wo, gate, up, down, ck, cv)
+    )(dealing, lengths, counts, parents, path, freq, gain, q, k, v, res, wo, gate, up, down, ck, cv)
 
 
 def mlp_kernel(
-    st_hbm, w_hbm, dn_hbm, gain_ref, out_ref,
-    S, W, DN, acc, H, ss, T, R, Q, T2, R2,
+    dealt_ref, st_hbm, w_hbm, dn_hbm, gain_ref, out_ref,
+    S, W, DN, acc, H, ss, T, R, Q, T2, R2, F, inverse,
     loc_sem, ag_send, ag_recv, rs_send, rs_recv, rt_send, rt_recv,
 ):
     me = lax.axis_index("col")
@@ -459,13 +471,6 @@
 
     acc[...] = jnp.zeros_like(acc)
     ss[...] = jnp.zeros_like(ss)
-    w_in.wait()
-
-    @pl.loop(0, 8)
-    def _(r):
-        both = jnp.concatenate([gain_ref[2 * r], gain_ref[2 * r + 1]], axis=1)
-        W[r] = W[r] * both.astype(jnp.bfloat16)
-
     for h in halves:
         arrived(h, 0, at(h, -1, 0))
         push(h, 2, at(h, -1, 0), peer1(h, 1), 0)
@@ -523,6 +528,20 @@
         arrived(h, 3, at(h, 2, 0), 96)
         push(h, 16, at(h, 2, 0), peer2(h, 1))
         push(h, 17, at(h, 2, 0), peer2(h, -1))
+    w_in.wait()
+
+    @pl.loop(0, 8)
+    def _(r):
+        both = jnp.concatenate([gain_ref[2 * r], gain_ref[2 * r + 1]], axis=1)
+        W[r] = W[r] * both.astype(jnp.bfloat16)
+
+    @pl.loop(0, 16)
+    def _(i):
+        slot = jnp.int32(0)
+        for j in range(16):
+            slot = jnp.where(dealt_ref[0, j] == i, j, slot)
+        inverse[i] = slot
+
     fold_a(z)
     second(1)
     second(2)
@@ -604,10 +623,6 @@
                 + R[h, s_kind, b % 2].astype(jnp.float32)
                 + R[h, d_kind, b % 2].astype(jnp.float32)
             ).astype(jnp.bfloat16)
-    for h in halves:
-        for i in range(2):
-            pass
-
     def copy2(h, kind, src, target):
         return pltpu.make_async_remote_copy(
             src_ref=src, dst_ref=R2.at[h, kind],
@@ -637,17 +652,26 @@
         for row, s_kind, d_kind in ((0, 2, 5), (96, 3, 4)):
             copy2(h, s_kind, T2.at[h, 0], me).wait_recv()
             copy2(h, d_kind, T2.at[h, 0], me).wait_recv()
-            out_ref[pl.ds(row, 96), pl.ds(512 * h, 512)] = (
+            rows = (
                 S[h, me, pl.ds(row, 96)].astype(jnp.float32)
                 + Q[h, b_own[h], pl.ds(row, 96)].astype(jnp.float32)
                 + R2[h, s_kind].astype(jnp.float32)
                 + R2[h, d_kind].astype(jnp.float32)
             ).astype(jnp.bfloat16)
+            for n in range(8):
+                F[8 * h + n, pl.ds(row, 96)] = rows[:, 64 * n : 64 * n + 64]
+
+    @pl.loop(0, 8)
+    def _(m):
+        out_ref[:, pl.ds(pl.multiple_of(m * 128, 128), 128)] = jnp.concatenate(
+            [F[inverse[2 * m]], F[inverse[2 * m + 1]]], axis=1
+        )
+
     for cp in sent:
         cp.wait_send()
 
 
-def mlp_call(stream_t, weights, down_t, gain):
+def mlp_call(dealing, stream_t, weights, down_t, gain):
     anyspace = pl.BlockSpec(memory_space=pl.ANY)
     vmem = pl.BlockSpec(memory_space=pltpu.VMEM)
     bf, f32 = jnp.bfloat16, jnp.float32
@@ -655,7 +679,7 @@
     return pl.pallas_call(
         mlp_kernel,
         out_shape=jax.ShapeDtypeStruct((192, 1024), bf),
-        in_specs=[anyspace, anyspace, anyspace, vmem],
+        in_specs=[pl.BlockSpec(memory_space=pltpu.SMEM), anyspace, anyspace, anyspace, vmem],
         out_specs=vmem,
         scratch_shapes=[
             pltpu.VMEM((2, 16, 192, 512), bf),
@@ -669,6 +693,8 @@
             pltpu.VMEM((2, 4, 192, 512), bf),
             pltpu.VMEM((2, 2, 96, 512), bf),
             pltpu.VMEM((2, 6, 96, 512), bf),
+            pltpu.VMEM((16, 192, 64), bf),
+            pltpu.SMEM((16,), jnp.int32),
             dma((4,)),
             dma((2, 20)),
             dma((2, 20)),
@@ -681,7 +707,7 @@
             collective_id=0, has_side_effects=True, vmem_limit_bytes=60 * 1024 * 1024
         ),
         name="mlp",
-    )(stream_t, weights, down_t, gain)
+    )(dealing, stream_t, weights, down_t, gain)
 
 
 def body(
@@ -704,32 +730,27 @@
 ):
     freq = np.power(10000.0, -(np.arange(192) % 48) * (2.0 / HEAD_DIM)).astype(np.float32)
 
-    def by_request(rows):
-        return rows.reshape(16, 64, 192)
-
     stream_t, new_keys, new_values, gains, gate_up, down_t = attend_call(
         dealing,
         cache_lengths,
         draft_counts,
-        parents.reshape(64, 1),
-        accepted.reshape(8, 1),
+        parents,
+        accepted,
         jnp.asarray(freq).reshape(1, 192),
-        norm_gain.reshape(1, 192),
-        by_request(queries),
-        by_request(draft_keys),
-        by_request(draft_values),
-        by_request(residual),
-        out_weight,
+        norm_gain,
+        queries.T,
+        draft_keys.T,
+        draft_values.T,
+        residual.T,
+        out_weight.T,
         gate_weight,
         up_weight,
         down_weight,
         cache_keys,
         cache_values,
     )
-    out_t = mlp_call(stream_t, gate_up, down_t.reshape(3072, 512), gains)
-    inverse = jnp.argsort(dealing[0])
-    layer_out = jnp.take(out_t.T.reshape(16, 64, 192), inverse, axis=0).reshape(1024, 192)
-    return (layer_out, new_keys, new_values)
+    out_t = mlp_call(dealing, stream_t, gate_up, down_t.reshape(3072, 512), gains)
+    return (out_t.T, new_keys, new_values)
 
 
 def solution(mesh):

time: 187 us -> 170 us (0.909)
  local copies, waits for them, and re-layouts: 17.8 us -> 3.02 us
    unnamed x14 -> x7, local copies, waits for them, and re-layouts: 11.9 us -> 3.02 us
    reshape x3 -> x0, local copies, waits for them, and re-layouts: 3.91 us -> none  [the longest x1 1.36 us: body(): parents.reshape(64, 1)]
where the time goes in v3:
time: 170 us
  Pallas kernels  165 us (97%)
  local copies, waits for them, and re-layouts  3.02 us (2%)
  between operations  1.96 us (1%)
    pallas_call x1, Pallas kernels, mlp_call(): pl.pallas_call(mlp_kernel, out_shape=jax.ShapeDtypeStruct((192, 1024), bf...  89.7 us
    pallas_call x1, Pallas kernels, attend_call(): pl.pallas_call(attend_kernel, out_shape=(jax.ShapeDtypeStruct((192, 1024)...  75 us

profile of v3, /device:TPU:0, one launch (start us, length us, event | category | flops | bytes accessed | tf_op | source)
XLA Modules:
  0.0 169.6 jit_solution(17675804311367204392)
XLA Ops:
  1.9 75.0 %attend.1 = (bf16[192,1024]{1,0:T(8,128)(2,1)}, bf16[1,8,3072]{2,1,0:T(8,128)(2,1)}, bf16[1,8,3072]{2,1,0:T(8,128)(2,1)}, f32[16,1,192]{2,1,0:T(1,128)}, bf16[8,...) custom-call(s32[1,16]{1,0:T(1,128)} %dealt_ref.3, s32[1]{0:T(128)S(6)} %copy.23.length_ref, s32[1]{0:T(128)S(6)} %copy.24.count_ref, ...), custom_call_target="tpu_custom_call" | custom-call | tf_op jit(solution)/shard_map/attend/pallas_call | solution.py:360
  76.9 0.0 copy-start.1
  76.9 0.0 copy-start
  77.0 89.7 %mlp.1 = bf16[192,1024]{1,0:T(8,128)(2,1)} custom-call(s32[1,16]{1,0:T(1,128)} %dealt_ref.3, bf16[192,1024]{1,0:T(8,128)(2,1)} %get-tuple-element.9.st_hbm, bf16[8,1024,384]{2,1,0:T(8,128)(2,1)} %get-tuple-element.10.w_hbm, bf16[3072,512]{1,0:T(8,128)(2,1)} %bitcast.7, f32[16,1,192]{2,1,0:T(1,128)} %get-tuple-element.12.gain_ref), custom_call_target="tpu_custom_call" | custom-call | tf_op jit(solution)/shard_map/mlp/pallas_call | solution.py:679
  166.6 1.8 %copy.25 = bf16[1024,192]{0,1:T(8,128)(2,1)} copy(bf16[1024,192]{0,1:T(8,128)(2,1)} %bitcast.8) | data formatting | bytes 786432
  168.4 0.0 copy-done.1
  168.4 0.6 copy.26
  169.0 0.0 copy-done
  169.0 0.6 copy.27
Async XLA Ops:
  76.9 91.5 %copy-start.1 = (bf16[1,8,3072]{2,1,0:T(8,128)(2,1)S(1)}, bf16[1,8,3072]{2,1,0:T(8,128)(2,1)}, u32[]{:S(2)}) copy-start(bf16[1,8,3072]{2,1,0:T(8,128)(2,1)} %get-tuple-element.19) | copy-start | bytes 147460
  76.9 92.1 %copy-start = (bf16[1,8,3072]{2,1,0:T(8,128)(2,1)S(1)}, bf16[1,8,3072]{2,1,0:T(8,128)(2,1)}, u32[]{:S(2)}) copy-start(bf16[1,8,3072]{2,1,0:T(8,128)(2,1)} %get-tuple-element.20) | copy-start | bytes 147460

commit v4 on v3

--- a/solution.py
+++ b/solution.py
@@ -41,11 +41,17 @@
     z, x = me // 4, me % 4
     y, core = row // 2, row % 2
 
-    def cache_in(p):
-        lanes = pl.ds(pl.multiple_of(p * 384, 128), 384)
+    def near(g):
+        return g + g // 2 - 2 * (g // 3)
+
+    def heads_at(i, zz):
+        return 2 * ((zz + near(i // 2)) % 4) + i % 2
+
+    def cache_in(i):
+        lanes = pl.ds(pl.multiple_of(heads_at(i, z) * 384, 128), 384)
         return (
-            pltpu.make_async_copy(ck_hbm.at[0, :, lanes], KC.at[p], kv_sem.at[0, p]),
-            pltpu.make_async_copy(cv_hbm.at[0, :, lanes], VC.at[p], kv_sem.at[1, p]),
+            pltpu.make_async_copy(ck_hbm.at[0, :, lanes], KC.at[i], kv_sem.at[0, i]),
+            pltpu.make_async_copy(cv_hbm.at[0, :, lanes], VC.at[i], kv_sem.at[1, i]),
         )
 
     @pl.loop(0, 8)
@@ -105,9 +111,12 @@
 
     @pl.loop(1, 16)
     def _(d):
-        j = (me + d) % 16
+        j = ((z + 4 - near(d // 4)) % 4) * 4 + (x + near(d % 4)) % 4
         block_copy(j).start()
-        gain_copy(j, me).start()
+
+    @pl.loop(1, 16)
+    def _(d):
+        gain_copy((me + d) % 16, me).start()
 
     WO[row] = wo_ref[...]
     TG[0:512] = gate_ref[...].astype(f32).T.astype(bf)
@@ -230,7 +239,8 @@
         (path_ref[...] == lax.broadcasted_iota(jnp.int32, (64, 8), 0)).astype(f32).T.astype(bf)
     )
 
-    def chunk(p, h):
+    def chunk(i, h):
+        p = heads_at(i, z)
         for e in range(2):
             @pl.when(2 * p + e != me)
             def _(e=e):
@@ -250,9 +260,9 @@
         wide = jnp.concatenate(
             [jnp.where(head_of_lane == n, q, jnp.zeros_like(q)) for n in range(4)], axis=0
         )
-        for c in cache_in(p):
+        for c in cache_in(i):
             c.wait()
-        old = lax.dot_general(wide, KC[p], nt, preferred_element_type=f32)
+        old = lax.dot_general(wide, KC[i], nt, preferred_element_type=f32)
         old = jnp.where(key_live, old, -jnp.inf)
         new = lax.dot_general(wide, kd, nt, preferred_element_type=f32)
         allowed = jnp.concatenate([anc_ref[...]] * 4, axis=0) > 0.5
@@ -263,16 +273,16 @@
         w_old = jnp.exp((old - top) * scale)
         w_new = jnp.exp((new - top) * scale)
         total = jnp.sum(w_old, axis=1, keepdims=True) + jnp.sum(w_new, axis=1, keepdims=True)
-        mixed = jnp.dot(w_old.astype(bf), VC[p], preferred_element_type=f32) + jnp.dot(
+        mixed = jnp.dot(w_old.astype(bf), VC[i], preferred_element_type=f32) + jnp.dot(
             w_new.astype(bf), vd, preferred_element_type=f32
         )
         mixed = mixed / total
         attended = jnp.zeros((64, 384), f32)
         for n in range(4):
             attended = jnp.where(head_of_lane == n, mixed[64 * n : 64 * n + 64], attended)
-        ATT[p, me] = attended.astype(bf)
+        ATT[i, me] = attended.astype(bf)
         for k in (0, 1, 4, 5):
-            amove(p, h, k).start()
+            amove(i, h, k).start()
 
     @pl.loop(0, 4)
     def _(g):
@@ -320,9 +330,11 @@
             p = 2 * g + h
             for k in (6, 7, 10, 11, 14, 15, 18, 19):
                 agot(p, h, k)
-            PA[...] += lax.dot_general(
-                WO[p], ATT[p].reshape(1024, 384), nt, preferred_element_type=f32
-            )
+            for zz in range(4):
+                PA[:, 256 * zz : 256 * zz + 256] += lax.dot_general(
+                    WO[heads_at(p, zz)], ATT[p, 4 * zz : 4 * zz + 4].reshape(256, 384), nt,
+                    preferred_element_type=f32,
+                )
 
     stream_ref[...] = PA[...].astype(bf)
     last(2)
@@ -406,8 +418,9 @@
 def mlp_kernel(
     dealt_ref, st_hbm, w_hbm, dn_hbm, gain_ref, out_ref,
     S, W, DN, acc, H, ss, T, R, Q, T2, R2, F, inverse,
-    loc_sem, ag_send, ag_recv, rs_send, rs_recv, rt_send, rt_recv,
+    st_sem, w_sem, ag_send, ag_recv, rs_send, rs_recv, rt_send, rt_recv,
 ):
+    f32, bf = jnp.float32, jnp.bfloat16
     me = lax.axis_index("col")
     z, x = me // 4, me % 4
     halves = (0, 1)
@@ -416,25 +429,31 @@
     def blk(h, a, b):
         return b * 4 + a if h == 0 else a * 4 + b
 
-    def peer1(h, d):
-        return blk(h, (a_own[h] + d + 4) % 4, b_own[h])
-
-    def peer2(h, d):
-        return blk(h, a_own[h], (b_own[h] + d + 4) % 4)
+    def at(h, da, db):
+        return blk(h, (a_own[h] + da + 4) % 4, (b_own[h] + db + 4) % 4)
+
+    def peer(h, axis, way):
+        return at(h, way, 0) if axis == 1 else at(h, 0, way)
 
     stream_in = [
-        pltpu.make_async_copy(st_hbm.at[:, pl.ds(512 * h, 512)], S.at[h, me], loc_sem.at[h])
+        pltpu.make_async_copy(
+            st_hbm.at[:, pl.ds(512 * t + 256 * h, 256)], S.at[t, h, me], st_sem.at[t, h]
+        )
+        for t in range(2)
         for h in halves
     ]
-    w_in = pltpu.make_async_copy(w_hbm, W, loc_sem.at[2])
-    dn_in = pltpu.make_async_copy(dn_hbm, DN, loc_sem.at[3])
-    for c in stream_in:
+    w_in = [
+        pltpu.make_async_copy(
+            w_hbm.at[r], W.at[r // 2, :, pl.ds(384 * (r % 2), 384)], w_sem.at[r]
+        )
+        for r in range(8)
+    ]
+    dn_in = pltpu.make_async_copy(dn_hbm, DN, w_sem.at[8])
+    for c in stream_in + w_in + [dn_in]:
         c.start()
-    w_in.start()
-    dn_in.start()
 
     barrier = pltpu.get_barrier_semaphore()
-    for p in (peer1(0, 1), peer1(0, -1), peer1(1, 1), peer1(1, -1)):
+    for p in (peer(0, 1, 1), peer(0, 1, -1), peer(0, 2, 1), peer(0, 2, -1)):
         pl.semaphore_signal(barrier, inc=1, device_id={"col": p}, device_id_type=MESH)
     pl.semaphore_wait(barrier, 4)
     for c in stream_in:
@@ -442,98 +461,200 @@
 
     sent = []
 
-    def push(h, k, c, target, rows=None):
-        ref = S.at[h, c] if rows is None else S.at[h, c, pl.ds(rows, 96)]
-        cp = pltpu.make_async_remote_copy(
-            src_ref=ref, dst_ref=ref, send_sem=ag_send.at[h, k], recv_sem=ag_recv.at[h, k],
-            device_id={"col": target}, device_id_type=MESH,
-        )
-        cp.start()
-        sent.append(cp)
-
-    def arrived(h, k, c, rows=None):
-        ref = S.at[h, c] if rows is None else S.at[h, c, pl.ds(rows, 96)]
-        pltpu.make_async_remote_copy(
-            src_ref=ref, dst_ref=ref, send_sem=ag_send.at[h, k], recv_sem=ag_recv.at[h, k],
-            device_id={"col": me}, device_id_type=MESH,
-        ).wait_recv()
-
-    def at(h, da, db):
-        return blk(h, (a_own[h] + da + 4) % 4, (b_own[h] + db + 4) % 4)
-
-    offs = (0, -1, 1, 2)
-    for h in halves:
-        push(h, 0, me, peer1(h, 1))
-        push(h, 1, me, peer1(h, -1))
-    for h in halves:
-        push(h, 4, me, peer2(h, 1))
-        push(h, 5, me, peer2(h, -1))
-
-    acc[...] = jnp.zeros_like(acc)
-    ss[...] = jnp.zeros_like(ss)
-    for h in halves:
-        arrived(h, 0, at(h, -1, 0))
-        push(h, 2, at(h, -1, 0), peer1(h, 1), 0)
-        push(h, 8, at(h, -1, 0), peer2(h, 1))
-        push(h, 9, at(h, -1, 0), peer2(h, -1))
-        arrived(h, 1, at(h, 1, 0))
-        push(h, 3, at(h, 1, 0), peer1(h, -1), 96)
-        push(h, 12, at(h, 1, 0), peer2(h, 1))
-        push(h, 13, at(h, 1, 0), peer2(h, -1))
-
-    def second(j):
-        for h in halves:
-            base = 4 + 4 * j
-            arrived(h, base, at(h, offs[j], -1))
-            push(h, base + 2, at(h, offs[j], -1), peer2(h, 1), 0)
-            arrived(h, base + 1, at(h, offs[j], 1))
-            push(h, base + 3, at(h, offs[j], 1), peer2(h, -1), 96)
-
-    def square(h, c):
-        v = S[h, c].astype(jnp.float32)
-        ss[h] += jnp.sum(v * v, axis=0, keepdims=True)
-
-    def fold_a(zz):
-        for i in range(4):
-            square(0, zz * 4 + i)
-        k0 = S[0, pl.ds(zz * 4, 2)].reshape(384, 512)
-        k1 = S[0, pl.ds(zz * 4 + 2, 2)].reshape(384, 512)
+    def gmove(t, h, k, offset):
+        (da, db), axis, way, part, landed = HOPS[k]
+        if offset == "landed":
+            da, db = landed
+        ref = S.at[t, h, at(h, da, db)]
+        if part is not None:
+            ref = S.at[t, h, at(h, da, db), pl.ds(96 * part, 96)]
+        return pltpu.make_async_remote_copy(
+            src_ref=ref, dst_ref=ref, send_sem=ag_send.at[t, h, k], recv_sem=ag_recv.at[t, h, k],
+            device_id={"col": peer(h, axis, way)}, device_id_type=MESH,
+        )
+
+    def push(t, h, *ks):
+        for k in ks:
+            cp = gmove(t, h, k, "sent")
+            cp.start()
+            sent.append(cp)
+
+    def got(t, h, *ks):
+        for k in ks:
+            gmove(t, h, k, "landed").wait_recv()
+
+    def gather0(t):
+        for h in halves:
+            push(t, h, 0, 1)
+        for h in halves:
+            push(t, h, 4, 5)
+
+    def gather1(t):
+        for h in halves:
+            got(t, h, 0)
+            push(t, h, 2, 8, 9)
+            got(t, h, 1)
+            push(t, h, 3, 12, 13)
+
+    def gather2(t):
+        for h in halves:
+            for k in (4, 5):
+                got(t, h, k)
+                push(t, h, k + 2)
+            got(t, h, 2, 3)
+            push(t, h, 16, 17)
+
+    def gather3(t):
+        for h in halves:
+            for k in (8, 9, 12, 13):
+                got(t, h, k)
+                push(t, h, k + 2)
+
+    def gather4(t):
+        for h in halves:
+            for k in (16, 17):
+                got(t, h, k)
+                push(t, h, k + 2)
+
+    def gather5(t):
+        for h in halves:
+            got(t, h, 6, 7, 10, 11, 14, 15, 18, 19)
+
+    def squares(t, h, v):
+        v = v.astype(f32)
+        ss[t, h] += jnp.sum(v * v, axis=0, keepdims=True)
+
+    def fold_a(t, zz):
+        k = S[t, 0, pl.ds(zz * 4, 4)].reshape(768, 256)
+        squares(t, 0, k)
 
         @pl.loop(0, 4)
         def _(m):
             rows = pl.ds(pl.multiple_of(m * 256, 256), 256)
-            acc[0, rows] += jnp.dot(
-                W[2 * zz, rows], k0, preferred_element_type=jnp.float32
-            ) + jnp.dot(W[2 * zz + 1, rows], k1, preferred_element_type=jnp.float32)
-
-    def fold_b(q):
-        @pl.loop(0, 2)
+            acc[t, 0, rows] += jnp.dot(W[zz, rows], k, preferred_element_type=f32)
+
+    def fold_b(t, q):
+        lanes = pl.ds(pl.multiple_of(q * 384, 128), 384)
+
+        @pl.loop(0, 4)
         def _(g):
-            for i in range(2):
-                for e in range(2):
-                    square(1, (2 * g + i) * 4 + 2 * q + e)
-            k0 = S[1, pl.ds(8 * g + 2 * q, 2)].reshape(384, 512)
-            k1 = S[1, pl.ds(8 * g + 4 + 2 * q, 2)].reshape(384, 512)
+            k = S[t, 1, pl.ds(4 * g + 2 * q, 2)].reshape(384, 256)
+            squares(t, 1, k)
 
             @pl.loop(0, 4)
             def _(m):
                 rows = pl.ds(pl.multiple_of(m * 256, 256), 256)
-                acc[1, rows] += jnp.dot(
-                    W[4 * g + q, rows], k0, preferred_element_type=jnp.float32
-                ) + jnp.dot(W[4 * g + 2 + q, rows], k1, preferred_element_type=jnp.float32)
-
-    second(0)
-    for h in halves:
-        arrived(h, 2, at(h, 2, 0), 0)
-        arrived(h, 3, at(h, 2, 0), 96)
-        push(h, 16, at(h, 2, 0), peer2(h, 1))
-        push(h, 17, at(h, 2, 0), peer2(h, -1))
-    w_in.wait()
-
-    @pl.loop(0, 8)
-    def _(r):
-        both = jnp.concatenate([gain_ref[2 * r], gain_ref[2 * r + 1]], axis=1)
-        W[r] = W[r] * both.astype(jnp.bfloat16)
+                acc[t, 1, rows] += jnp.dot(W[g, rows, lanes], k, preferred_element_type=f32)
+
+    def activate(t):
+        for h in halves:
+            factor = lax.rsqrt(ss[t, h] * (1.0 / D) + 1e-05)
+
+            @pl.loop(0, 4)
+            def _(m, h=h, factor=factor):
+                rows = pl.ds(pl.multiple_of(m * 128, 128), 128)
+                uprows = pl.ds(pl.multiple_of(512 + m * 128, 128), 128)
+                g = acc[t, h, rows] * factor
+                u = acc[t, h, uprows] * factor
+                H[t, h, rows] = (g / (1.0 + jnp.exp(-g)) * u).astype(bf)
+
+    def parts(t, h, da, b0):
+        rows = []
+        for b in (b0, b0 + 1):
+            c = blk(h, (a_own[h] + da + 4) % 4, b)
+            rows.append(DN[pl.ds(pl.multiple_of(c * 192, 192), 192)])
+        return jnp.dot(
+            jnp.concatenate(rows, axis=0), H[t, h], preferred_element_type=f32
+        ).reshape(2, 192, 256)
+
+    def smove(t, h, kind):
+        return pltpu.make_async_remote_copy(
+            src_ref=T.at[t, h, kind], dst_ref=R.at[t, h, kind],
+            send_sem=rs_send.at[t, h, kind], recv_sem=rs_recv.at[t, h, kind],
+            device_id={"col": peer(h, 1, 1 if kind % 2 == 0 else -1)}, device_id_type=MESH,
+        )
+
+    def sum1(t):
+        for kind, da, b0 in ((0, 2, 0), (1, 2, 2), (4, 1, 2), (5, -1, 0)):
+            for h in halves:
+                T[t, h, kind] = parts(t, h, da, b0).astype(bf)
+                cp = smove(t, h, kind)
+                cp.start()
+                sent.append(cp)
+
+    def sum2(t):
+        for kind, da, b0 in ((2, 1, 0), (3, -1, 2)):
+            for h in halves:
+                mine = parts(t, h, da, b0)
+                smove(t, h, kind - 2).wait_recv()
+                T[t, h, kind] = (mine + R[t, h, kind - 2].astype(f32)).astype(bf)
+                cp = smove(t, h, kind)
+                cp.start()
+                sent.append(cp)
+
+    def bmod(h, d):
+        return (b_own[h] + d + 4) % 4
+
+    def qmove(t, h, kind, src):
+        return pltpu.make_async_remote_copy(
+            src_ref=src, dst_ref=R2.at[t, h, kind],
+            send_sem=rt_send.at[t, h, kind], recv_sem=rt_recv.at[t, h, kind],
+            device_id={"col": peer(h, 2, 1 if kind % 2 == 0 else -1)}, device_id_type=MESH,
+        )
+
+    def sum3(t):
+        for b0, s_kind, d_kind in ((0, 2, 5), (2, 3, 4)):
+            for h in halves:
+                mine = parts(t, h, 0, b0)
+                smove(t, h, s_kind).wait_recv()
+                smove(t, h, d_kind).wait_recv()
+                Q[t, h, b0 : b0 + 2] = (
+                    mine + R[t, h, s_kind].astype(f32) + R[t, h, d_kind].astype(f32)
+                ).astype(bf)
+        for h in halves:
+            for kind, d, row in ((0, 2, 0), (1, 2, 96), (4, 1, 96), (5, -1, 0)):
+                cp = qmove(t, h, kind, Q.at[t, h, bmod(h, d), pl.ds(row, 96)])
+                cp.start()
+                sent.append(cp)
+
+    def sum4(t):
+        for h in halves:
+            for kind, d, row in ((2, 1, 0), (3, -1, 96)):
+                qmove(t, h, kind - 2, T2.at[t, h, 0]).wait_recv()
+                T2[t, h, kind - 2] = (
+                    Q[t, h, bmod(h, d), pl.ds(row, 96)].astype(f32)
+                    + R2[t, h, kind - 2].astype(f32)
+                ).astype(bf)
+                cp = qmove(t, h, kind, T2.at[t, h, kind - 2])
+                cp.start()
+                sent.append(cp)
+
+    def sum5(t):
+        for h in halves:
+            for row, s_kind, d_kind in ((0, 2, 5), (96, 3, 4)):
+                qmove(t, h, s_kind, T2.at[t, h, 0]).wait_recv()
+                qmove(t, h, d_kind, T2.at[t, h, 0]).wait_recv()
+                rows = (
+                    S[t, h, me, pl.ds(row, 96)].astype(f32)
+                    + Q[t, h, b_own[h], pl.ds(row, 96)].astype(f32)
+                    + R2[t, h, s_kind].astype(f32)
+                    + R2[t, h, d_kind].astype(f32)
+                ).astype(bf)
+                for n in range(4):
+                    F[8 * t + 4 * h + n, pl.ds(row, 96)] = rows[:, 64 * n : 64 * n + 64]
+
+    gather0(0)
+    acc[...] = jnp.zeros_like(acc)
+    ss[...] = jnp.zeros_like(ss)
+    gather1(0)
+    gather0(1)
+    for c in w_in:
+        c.wait()
+
+    @pl.loop(0, 4)
+    def _(g):
+        gains = jnp.concatenate([gain_ref[4 * g + n] for n in range(4)], axis=1).astype(bf)
+        W[g] = W[g] * gains
 
     @pl.loop(0, 16)
     def _(i):
@@ -542,124 +663,40 @@
             slot = jnp.where(dealt_ref[0, j] == i, j, slot)
         inverse[i] = slot
 
-    fold_a(z)
-    second(1)
-    second(2)
-    second(3)
-
-    @pl.loop(0, 2)
-    def _(i):
-        fold_a((z + 3 + 2 * i) % 4)
-
-    fold_b(x // 2)
-    for h in halves:
-        for j in range(4):
-            arrived(h, 6 + 4 * j, at(h, offs[j], 2), 0)
-            arrived(h, 7 + 4 * j, at(h, offs[j], 2), 96)
-    fold_a((z + 2) % 4)
-    fold_b(1 - x // 2)
-    for cp in sent:
-        cp.wait_send()
-
-    for h in halves:
-        factor = lax.rsqrt(ss[h] * (1.0 / D) + 1e-05)
-
-        @pl.loop(0, 4)
-        def _(m, h=h, factor=factor):
-            rows = pl.ds(pl.multiple_of(m * 128, 128), 128)
-            uprows = pl.ds(pl.multiple_of(512 + m * 128, 128), 128)
-            g = acc[h, rows] * factor
-            u = acc[h, uprows] * factor
-            H[h, rows] = (g / (1.0 + jnp.exp(-g)) * u).astype(jnp.bfloat16)
-
+    gather2(0)
+    fold_a(0, z)
+    gather3(0)
+    gather1(1)
+    gather4(0)
+    fold_a(0, (z + 3) % 4)
+    fold_a(0, (z + 1) % 4)
+    fold_b(0, x // 2)
+    gather2(1)
+    gather5(0)
+    fold_a(0, (z + 2) % 4)
+    fold_b(0, 1 - x // 2)
+    gather3(1)
+    activate(0)
+    gather4(1)
     dn_in.wait()
-
-    def part(h, c):
-        rows = pl.ds(pl.multiple_of(c * 192, 192), 192)
-        return jnp.dot(DN[rows], H[h], preferred_element_type=jnp.float32)
-
-    sent = []
-
-    def send1(h, kind, i):
-        d = 1 if kind % 2 == 0 else -1
-        cp = pltpu.make_async_remote_copy(
-            src_ref=T.at[h, kind, i], dst_ref=R.at[h, kind, i],
-            send_sem=rs_send.at[h, kind, i], recv_sem=rs_recv.at[h, kind, i],
-            device_id={"col": peer1(h, d)}, device_id_type=MESH,
-        )
-        cp.start()
-        sent.append(cp)
-
-    def got1(h, kind, i):
-        pltpu.make_async_remote_copy(
-            src_ref=T.at[h, kind, i], dst_ref=R.at[h, kind, i],
-            send_sem=rs_send.at[h, kind, i], recv_sem=rs_recv.at[h, kind, i],
-            device_id={"col": me}, device_id_type=MESH,
-        ).wait_recv()
-
-    def dest(h, da, b):
-        return blk(h, (a_own[h] + da + 4) % 4, b)
-
-    for kind, da, b0 in ((0, 2, 0), (1, 2, 2), (4, 1, 2), (5, -1, 0)):
-        for i in range(2):
-            for h in halves:
-                T[h, kind, i] = part(h, dest(h, da, b0 + i)).astype(jnp.bfloat16)
-                send1(h, kind, i)
-    for kind, da, b0 in ((2, 1, 0), (3, -1, 2)):
-        for i in range(2):
-            for h in halves:
-                mine = part(h, dest(h, da, b0 + i))
-                got1(h, kind - 2, i)
-                T[h, kind, i] = (mine + R[h, kind - 2, i].astype(jnp.float32)).astype(jnp.bfloat16)
-                send1(h, kind, i)
-    for b in range(4):
-        for h in halves:
-            mine = part(h, dest(h, 0, b))
-            s_kind, d_kind = (2, 5) if b < 2 else (3, 4)
-            got1(h, s_kind, b % 2)
-            got1(h, d_kind, b % 2)
-            Q[h, b] = (
-                mine
-                + R[h, s_kind, b % 2].astype(jnp.float32)
-                + R[h, d_kind, b % 2].astype(jnp.float32)
-            ).astype(jnp.bfloat16)
-    def copy2(h, kind, src, target):
-        return pltpu.make_async_remote_copy(
-            src_ref=src, dst_ref=R2.at[h, kind],
-            send_sem=rt_send.at[h, kind], recv_sem=rt_recv.at[h, kind],
-            device_id={"col": target}, device_id_type=MESH,
-        )
-
-    def bmod(h, d):
-        return (b_own[h] + d + 4) % 4
-
-    for h in halves:
-        for kind, d, row in ((0, 2, 0), (1, 2, 96), (4, 1, 96), (5, -1, 0)):
-            cp = copy2(h, kind, Q.at[h, bmod(h, d), pl.ds(row, 96)], peer2(h, 1 if kind % 2 == 0 else -1))
-            cp.start()
-            sent.append(cp)
-    for h in halves:
-        for kind, d, row in ((2, 1, 0), (3, -1, 96)):
-            copy2(h, kind - 2, T2.at[h, 0], me).wait_recv()
-            T2[h, kind - 2] = (
-                Q[h, bmod(h, d), pl.ds(row, 96)].astype(jnp.float32)
-                + R2[h, kind - 2].astype(jnp.float32)
-            ).astype(jnp.bfloat16)
-            cp = copy2(h, kind, T2.at[h, kind - 2], peer2(h, 1 if kind == 2 else -1))
-            cp.start()
-            sent.append(cp)
-    for h in halves:
-        for row, s_kind, d_kind in ((0, 2, 5), (96, 3, 4)):
-            copy2(h, s_kind, T2.at[h, 0], me).wait_recv()
-            copy2(h, d_kind, T2.at[h, 0], me).wait_recv()
-            rows = (
-                S[h, me, pl.ds(row, 96)].astype(jnp.float32)
-                + Q[h, b_own[h], pl.ds(row, 96)].astype(jnp.float32)
-                + R2[h, s_kind].astype(jnp.float32)
-                + R2[h, d_kind].astype(jnp.float32)
-            ).astype(jnp.bfloat16)
-            for n in range(8):
-                F[8 * h + n, pl.ds(row, 96)] = rows[:, 64 * n : 64 * n + 64]
+    sum1(0)
+    fold_a(1, z)
+    fold_a(1, (z + 3) % 4)
+    fold_a(1, (z + 1) % 4)
+    fold_b(1, x // 2)
+    sum2(0)
+    gather5(1)
+    fold_a(1, (z + 2) % 4)
+    fold_b(1, 1 - x // 2)
+    activate(1)
+    sum1(1)
+    sum3(0)
+    sum2(1)
+    sum4(0)
+    sum3(1)
+    sum5(0)
+    sum4(1)
+    sum5(1)
 
     @pl.loop(0, 8)
     def _(m):
@@ -682,26 +719,27 @@
         in_specs=[pl.BlockSpec(memory_space=pltpu.SMEM), anyspace, anyspace, anyspace, vmem],
         out_specs=vmem,
         scratch_shapes=[
-            pltpu.VMEM((2, 16, 192, 512), bf),
-            pltpu.VMEM((8, 1024, 384), bf),
+            pltpu.VMEM((2, 2, 16, 192, 256), bf),
+            pltpu.VMEM((4, 1024, 768), bf),
             pltpu.VMEM((3072, 512), bf),
-            pltpu.VMEM((2, 1024, 512), f32),
-            pltpu.VMEM((2, 512, 512), bf),
-            pltpu.VMEM((2, 1, 512), f32),
-            pltpu.VMEM((2, 6, 2, 192, 512), bf),
-            pltpu.VMEM((2, 6, 2, 192, 512), bf),
-            pltpu.VMEM((2, 4, 192, 512), bf),
-            pltpu.VMEM((2, 2, 96, 512), bf),
-            pltpu.VMEM((2, 6, 96, 512), bf),
+            pltpu.VMEM((2, 2, 1024, 256), f32),
+            pltpu.VMEM((2, 2, 512, 256), bf),
+            pltpu.VMEM((2, 2, 1, 256), f32),
+            pltpu.VMEM((2, 2, 6, 2, 192, 256), bf),
+            pltpu.VMEM((2, 2, 6, 2, 192, 256), bf),
+            pltpu.VMEM((2, 2, 4, 192, 256), bf),
+            pltpu.VMEM((2, 2, 2, 96, 256), bf),
+            pltpu.VMEM((2, 2, 6, 96, 256), bf),
             pltpu.VMEM((16, 192, 64), bf),
             pltpu.SMEM((16,), jnp.int32),
-            dma((4,)),
-            dma((2, 20)),
-            dma((2, 20)),
-            dma((2, 6, 2)),
-            dma((2, 6, 2)),
-            dma((2, 6)),
-            dma((2, 6)),
+            dma((2, 2)),
+            dma((9,)),
+            dma((2, 2, 20)),
+            dma((2, 2, 20)),
+            dma((2, 2, 6)),
+            dma((2, 2, 6)),
+            dma((2, 2, 6)),
+            dma((2, 2, 6)),
         ],
         compiler_params=pltpu.CompilerParams(
             collective_id=0, has_side_effects=True, vmem_limit_bytes=60 * 1024 * 1024

time: 170 us -> 158 us (0.929)
  Pallas kernels: 165 us -> 152 us
    pallas_call x1, Pallas kernels: 75 us -> 66.2 us  [attend_call(): pl.pallas_call(attend_kernel, out_shape=(jax.ShapeDtypeStruct((192, 1024)...]
    pallas_call x1, Pallas kernels: 89.7 us -> 86.2 us  [mlp_call(): pl.pallas_call(mlp_kernel, out_shape=jax.ShapeDtypeStruct((192, 1024), bf...]
where the time goes in v4:
time: 158 us; the launch traced here: 157 us
  Pallas kernels  152 us (96%)
  local copies, waits for them, and re-layouts  3.02 us (2%)
  between operations  1.96 us (1%)
    pallas_call x1, Pallas kernels, mlp_call(): pl.pallas_call(mlp_kernel, out_shape=jax.ShapeDtypeStruct((192, 1024), bf...  86.2 us
    pallas_call x1, Pallas kernels, attend_call(): pl.pallas_call(attend_kernel, out_shape=(jax.ShapeDtypeStruct((192, 1024)...  66.2 us

profile of v4, /device:TPU:0, one launch (start us, length us, event | category | flops | bytes accessed | tf_op | source)
XLA Modules:
  0.0 157.4 jit_solution(409128076612677039)
XLA Ops:
  1.9 66.2 %attend.1 = (bf16[192,1024]{1,0:T(8,128)(2,1)}, bf16[1,8,3072]{2,1,0:T(8,128)(2,1)}, bf16[1,8,3072]{2,1,0:T(8,128)(2,1)}, f32[16,1,192]{2,1,0:T(1,128)}, bf16[8,...) custom-call(s32[1,16]{1,0:T(1,128)} %dealt_ref.3, s32[1]{0:T(128)S(6)} %copy.23.length_ref, s32[1]{0:T(128)S(6)} %copy.24.count_ref, ...), custom_call_target="tpu_custom_call" | custom-call | tf_op jit(solution)/shard_map/attend/pallas_call | solution.py:372
  68.1 0.0 copy-start.1
  68.1 0.0 copy-start
  68.1 86.2 %mlp.1 = bf16[192,1024]{1,0:T(8,128)(2,1)} custom-call(s32[1,16]{1,0:T(1,128)} %dealt_ref.3, bf16[192,1024]{1,0:T(8,128)(2,1)} %get-tuple-element.9.st_hbm, bf16[8,1024,384]{2,1,0:T(8,128)(2,1)} %get-tuple-element.10.w_hbm, bf16[3072,512]{1,0:T(8,128)(2,1)} %bitcast.7, f32[16,1,192]{2,1,0:T(1,128)} %get-tuple-element.12.gain_ref), custom_call_target="tpu_custom_call" | custom-call | tf_op jit(solution)/shard_map/mlp/pallas_call | solution.py:716
  154.4 1.8 %copy.25 = bf16[1024,192]{0,1:T(8,128)(2,1)} copy(bf16[1024,192]{0,1:T(8,128)(2,1)} %bitcast.8) | data formatting | bytes 786432
  156.1 0.0 copy-done.1
  156.1 0.6 copy.26
  156.8 0.0 copy-done
  156.8 0.6 copy.27
Async XLA Ops:
  68.1 88.0 %copy-start.1 = (bf16[1,8,3072]{2,1,0:T(8,128)(2,1)S(1)}, bf16[1,8,3072]{2,1,0:T(8,128)(2,1)}, u32[]{:S(2)}) copy-start(bf16[1,8,3072]{2,1,0:T(8,128)(2,1)} %get-tuple-element.19) | copy-start | bytes 147460
  68.1 88.6 %copy-start = (bf16[1,8,3072]{2,1,0:T(8,128)(2,1)S(1)}, bf16[1,8,3072]{2,1,0:T(8,128)(2,1)}, u32[]{:S(2)}) copy-start(bf16[1,8,3072]{2,1,0:T(8,128)(2,1)} %get-tuple-element.20) | copy-start | bytes 147460
